TPU v7x, 32 devices: a whole 2x2x4 slice. The times are simulated.
32 devices in a mesh: dp: 8 (over y, x, core), tensor: 4 (over z).
Axes of the slice: x: 2, y: 2, z: 4, core: 2. Of those that a mesh axis runs over, the one named last changes fastest.
Arguments:
- x_in: bfloat16 [2048, 768], P(('dp', 'tensor')), may hold values from -6 to 6
- segment_ids: int32 [2048], P('dp'), may hold values from 0 to 2, as said below
- norm_gain: float32 [2, 768], replicated, may hold values from 0.1 to 1.9
- w_zx: bfloat16 [2, 768, 2, 1536], P(None, 'dp', None, 'tensor'), may hold values from -0.21875 to 0.21875
- w_dt: bfloat16 [2, 768, 24], P(None, 'dp', 'tensor'), may hold values from -0.21875 to 0.21875
- w_bc: bfloat16 [2, 768, 256], P(None, 'dp'), may hold values from -0.21875 to 0.21875
- conv_x: float32 [2, 4, 1536], P(None, None, 'tensor'), may hold values from -3 to 3
- conv_x_bias: float32 [2, 1536], P(None, 'tensor'), may hold values from -2 to 2
- conv_bc: float32 [2, 4, 256], replicated, may hold values from -3 to 3
- conv_bc_bias: float32 [2, 256], replicated, may hold values from -2 to 2
- dt_bias: float32 [2, 24], P(None, 'tensor'), may hold values from -7 to -2
- a_log: float32 [2, 24], P(None, 'tensor'), may hold values from 0 to 1.5
- d_skip: float32 [2, 24], P(None, 'tensor'), may hold values from 0.5 to 1.5
- gate_gain: float32 [2, 1536], P(None, 'tensor'), may hold values from 0.1 to 1.9
- w_out: bfloat16 [2, 1536, 768], P(None, 'tensor', 'dp'), may hold values from -0.15625 to 0.15625
- cotangent: bfloat16 [2048, 768], P(('dp', 'tensor')), may hold values from -6 to 6
Outputs:
- y_out: bfloat16 [2048, 768], P(('dp', 'tensor'))
- d_x_in: float32 [2048, 768], P(('dp', 'tensor'))
- d_norm_gain: float32 [2, 768], replicated
- d_w_zx: float32 [2, 768, 2, 1536], P(None, 'dp', None, 'tensor')
- d_w_dt: float32 [2, 768, 24], P(None, 'dp', 'tensor')
- d_w_bc: float32 [2, 768, 256], P(None, 'dp')
- d_conv_x: float32 [2, 4, 1536], replicated
- d_conv_x_bias: float32 [2, 1536], replicated
- d_conv_bc: float32 [2, 4, 256], replicated
- d_conv_bc_bias: float32 [2, 256], replicated
- d_dt_bias: float32 [2, 24], replicated
- d_a_log: float32 [2, 24], replicated
- d_d_skip: float32 [2, 24], replicated
- d_gate_gain: float32 [2, 1536], replicated
- d_w_out: float32 [2, 1536, 768], P(None, 'tensor', 'dp')
Inputs may be any that keep to these rules, and one draw needn't show every extreme that they name: `segment_ids`: segment numbers start at 0 and rise by one at each new sequence; every sequence but the first and the last has exactly 1024 tokens, the first has 1 to 1023 tokens.
All inputs are finite; a program needn't handle non-finite values.
Results may differ from a plain program's by a relative error of at most 0.012.
The roundings to bfloat16 on the way count: a program that leaves them out, or rounds other values in their place, can miss the bound.
Values may be sent and summed in bfloat16 or wider, within the bound.
A program may use at most 128 MiB of HBM per device.

v0:
```python
from functools import partial

import jax
import jax.numpy as jnp
from jax import lax
from jax.sharding import PartitionSpec as P

STRETCH = 256


EPSILON = 1e-05
PRECISE = lax.Precision.HIGHEST


def entering(part, axis, combine, identity, reverse):
    count = lax.axis_size(axis)
    place = lax.axis_index(axis)
    ahead = count - 1 - place if reverse else place
    gathered = jax.tree.map(lambda a: lax.all_gather(a, axis), part)
    state = jax.tree.map(lambda a, e: jnp.zeros_like(a) + jnp.asarray(e, a.dtype), part, identity)

    def one(step, state):
        source = count - 1 - step if reverse else step
        return combine(
            state, jax.tree.map(lambda a: lax.dynamic_index_in_dim(a, source, 0, False), gathered)
        )

    return lax.fori_loop(0, ahead, one, state)


def passed_along(block, axis, distance):
    devices = range(lax.axis_size(axis))
    route = [(i - distance, i) for i in devices if i - distance in devices]
    return lax.ppermute(block, axis, route)


def stretch_core(
    xs_block, b_block, c_block, dt_block, la_block, skip_gain, seg_block, seg_before, state_in
):
    cumulative = jnp.cumsum(la_block, axis=0)
    length = seg_block.shape[0]
    places = jnp.arange(length)
    inside = (seg_block[:, None] == seg_block[None, :]) & (places[:, None] >= places[None, :])
    span_logs = cumulative[:, None, :] - cumulative[None, :, :]
    decays = jnp.exp(jnp.where(inside[:, :, None], span_logs, -1e30))
    scores = jnp.dot(c_block, b_block.T, precision=PRECISE)
    scaled = xs_block * dt_block[:, :, None]
    output = jnp.einsum("ijh,ij,jhp->ihp", decays, scores, scaled, precision=PRECISE)
    reached = (seg_block == seg_before).astype(jnp.float32)
    carried = jnp.einsum("in,hpn->ihp", c_block, state_in, precision=PRECISE)
    output = output + jnp.exp(cumulative)[:, :, None] * reached[:, None, None] * carried
    output = output + skip_gain[None, :, None] * xs_block
    last_seg = seg_block[length - 1]
    kept_rows = (seg_block == last_seg).astype(jnp.float32)
    to_end = jnp.exp(cumulative[length - 1][None, :] - cumulative) * kept_rows[:, None]
    whole_seg = (last_seg == seg_before).astype(jnp.float32)
    new_state = (whole_seg * jnp.exp(cumulative[length - 1]))[:, None, None] * state_in
    new_state = new_state + jnp.einsum("jh,jhp,jn->hpn", to_end, scaled, b_block, precision=PRECISE)
    return (output, new_state)


def conv_apply(extended, seg_extended, segments, conv_weight, conv_bias):
    length = segments.shape[0]
    tap_count = conv_weight.shape[0]
    result = jnp.zeros((length, extended.shape[1]), jnp.float32) + conv_bias
    for tap_index in range(tap_count):
        same_seg = (seg_extended[tap_index : tap_index + length] == segments).astype(jnp.float32)
        result = (
            result
            + conv_weight[tap_index] * extended[tap_index : tap_index + length] * same_seg[:, None]
        )
    return result


def mixer_front(
    extended,
    proj_dt,
    conv_weight,
    conv_bias,
    bias_dt,
    log_rate,
    seg_extended,
    segments,
    head_count,
    inner_width,
):
    activated = jax.nn.silu(conv_apply(extended, seg_extended, segments, conv_weight, conv_bias))
    length = segments.shape[0]
    state_width = (activated.shape[1] - inner_width) // 2
    xs_heads = activated[:, :inner_width].reshape(length, head_count, inner_width // head_count)
    b_mat = activated[:, inner_width : inner_width + state_width]
    c_mat = activated[:, inner_width + state_width :]
    step_dt = jax.nn.softplus(proj_dt + bias_dt)
    log_decay = -step_dt * jnp.exp(log_rate)
    return (xs_heads, b_mat, c_mat, step_dt, log_decay)


def mixer_core(xs_heads, b_mat, c_mat, step_dt, log_decay, skip_gain, segments, block_rows):
    length = segments.shape[0]
    block_count = length // block_rows
    head_count = xs_heads.shape[1]
    head_width = xs_heads.shape[2]
    state_width = b_mat.shape[1]
    before = jnp.concatenate([jnp.full((1,), -1, jnp.int32), segments[:-1]])
    firsts = before.reshape(block_count, block_rows)[:, 0]

    def advance(state_in, pieces):
        xs_block, b_block, c_block, dt_block, la_block, seg_block, seg_first = pieces
        output, state_out = stretch_core(
            xs_block,
            b_block,
            c_block,
            dt_block,
            la_block,
            skip_gain,
            seg_block,
            seg_first,
            state_in,
        )
        return (state_out, output)

    start_state = jnp.zeros((head_count, head_width, state_width), jnp.float32)
    final_state, outputs = lax.scan(
        advance,
        start_state,
        (
            xs_heads.reshape(block_count, block_rows, head_count, head_width),
            b_mat.reshape(block_count, block_rows, state_width),
            c_mat.reshape(block_count, block_rows, state_width),
            step_dt.reshape(block_count, block_rows, head_count),
            log_decay.reshape(block_count, block_rows, head_count),
            segments.reshape(block_count, block_rows),
            firsts,
        ),
    )
    return (outputs.reshape(length, head_count, head_width), final_state)


def init_output(log_decay, c_mat, start_state, segments):
    cumulative = jnp.cumsum(log_decay, axis=0)
    reached = (segments == segments[0]).astype(jnp.float32)
    carried = jnp.einsum("tn,hpn->thp", c_mat, start_state, precision=PRECISE)
    return jnp.exp(cumulative)[:, :, None] * reached[:, None, None] * carried


def init_carry(log_decay, start_state, segments):
    whole_seg = (segments[segments.shape[0] - 1] == segments[0]).astype(jnp.float32)
    return (whole_seg * jnp.exp(jnp.sum(log_decay, axis=0)))[:, None, None] * start_state


def pass_state(coefficient, values, backward):

    def combine(earlier, later):
        return (earlier[0] * later[0], later[1] + later[0][:, None, None] * earlier[1])

    identity = (jnp.ones_like(coefficient), jnp.zeros_like(values))
    prefix = entering((coefficient, values), "dp", combine, identity, backward)
    return prefix[1]


def spread(part, tensor_rank, tensor_count):
    total_width = part.shape[-1] * tensor_count
    blank = jnp.zeros(part.shape[:-1] + (total_width,), jnp.float32)
    return lax.dynamic_update_slice_in_dim(blank, part, tensor_rank * part.shape[-1], part.ndim - 1)


def local(
    x_in,
    segment_ids,
    norm_gain,
    w_zx,
    w_dt,
    w_bc,
    conv_x,
    conv_x_bias,
    conv_bc,
    conv_bc_bias,
    dt_bias,
    a_log,
    d_skip,
    gate_gain,
    w_out,
    cotangent,
):
    layers = norm_gain.shape[0]
    tensor_rank = lax.axis_index("tensor")
    tensor_count = lax.axis_size("tensor")
    model_width = x_in.shape[1]
    shard_rows = segment_ids.shape[0]
    local_inner = conv_x.shape[2]
    local_heads = dt_bias.shape[1]
    head_width = local_inner // local_heads
    full_inner = local_inner * tensor_count
    margin = conv_x.shape[1] - 1
    block_rows = min(STRETCH, shard_rows)

    def fetch(layer_num):
        return (
            lax.all_gather(w_zx[layer_num], "dp", axis=0, tiled=True),
            lax.all_gather(w_dt[layer_num], "dp", axis=0, tiled=True),
            lax.all_gather(w_bc[layer_num], "dp", axis=0, tiled=True),
            lax.all_gather(w_out[layer_num], "dp", axis=1, tiled=True),
        )

    hidden = x_in.astype(jnp.float32)
    records = []
    for layer_num in range(layers):
        weights = fetch(layer_num)
        zx_full, dt_full, bc_full, out_full = weights
        rms_scale = lax.rsqrt(jnp.mean(hidden * hidden, axis=1, keepdims=True) + EPSILON)
        normed = (hidden * rms_scale * norm_gain[layer_num]).astype(jnp.bfloat16)
        gathered = lax.all_gather(normed, "tensor", axis=0, tiled=True)
        proj_zx = jnp.dot(
            gathered,
            zx_full.reshape(model_width, 2 * local_inner),
            preferred_element_type=jnp.float32,
        )
        proj_z = proj_zx[:, :local_inner]
        proj_dt = jnp.dot(gathered, dt_full, preferred_element_type=jnp.float32)
        proj_bc = jnp.dot(gathered, bc_full, preferred_element_type=jnp.float32)
        conv_in = jnp.concatenate([proj_zx[:, local_inner:], proj_bc], axis=1).astype(jnp.bfloat16)
        seg_tail = (segment_ids[shard_rows - margin :] + 1).astype(jnp.bfloat16)
        tail_rows, tail_segs = passed_along((conv_in[shard_rows - margin :], seg_tail), "dp", 1)
        extended = jnp.concatenate([tail_rows, conv_in], axis=0).astype(jnp.float32)
        seg_extended = jnp.concatenate([tail_segs.astype(jnp.int32) - 1, segment_ids])
        joined = (seg_extended[margin - 1] == segment_ids[0]).astype(jnp.float32)
        conv_weight = jnp.concatenate([conv_x[layer_num], conv_bc[layer_num]], axis=1)
        conv_bias = jnp.concatenate([conv_x_bias[layer_num], conv_bc_bias[layer_num]])
        front_fn = partial(
            mixer_front,
            seg_extended=seg_extended,
            segments=segment_ids,
            head_count=local_heads,
            inner_width=local_inner,
        )
        xs_heads, b_mat, c_mat, step_dt, log_decay = front_fn(
            extended, proj_dt, conv_weight, conv_bias, dt_bias[layer_num], a_log[layer_num]
        )
        local_y, local_state = mixer_core(
            xs_heads, b_mat, c_mat, step_dt, log_decay, d_skip[layer_num], segment_ids, block_rows
        )
        whole_seg = (segment_ids[shard_rows - 1] == segment_ids[0]).astype(jnp.float32)
        coefficient = joined * whole_seg * jnp.exp(jnp.sum(log_decay, axis=0))
        incoming = pass_state(coefficient, local_state, False)
        start_state = joined * incoming
        ssd_y = (local_y + init_output(log_decay, c_mat, start_state, segment_ids)).reshape(
            shard_rows, local_inner
        )
        gated_y = ssd_y * jax.nn.silu(proj_z)
        squares = lax.psum(jnp.sum(gated_y * gated_y, axis=1), "tensor")
        inverse = lax.rsqrt(squares / full_inner + EPSILON)
        mixed_out = (gated_y * inverse[:, None] * gate_gain[layer_num]).astype(jnp.bfloat16)
        branch = lax.psum_scatter(
            jnp.dot(mixed_out, out_full, preferred_element_type=jnp.float32),
            "tensor",
            scatter_dimension=0,
            tiled=True,
        )
        records.append(
            (
                weights,
                hidden,
                gathered,
                proj_z,
                proj_dt,
                extended,
                seg_extended,
                joined,
                start_state,
                inverse,
            )
        )
        hidden = hidden + branch
    y_out = hidden.astype(jnp.bfloat16)
    grad_hidden = cotangent.astype(jnp.float32)
    layer_results = [None] * layers
    for layer_num in reversed(range(layers)):
        (
            weights,
            hidden_in,
            gathered,
            proj_z,
            proj_dt,
            extended,
            seg_extended,
            joined,
            start_state,
            inverse,
        ) = records[layer_num]
        zx_full, dt_full, bc_full, out_full = fetch(layer_num)
        conv_weight = jnp.concatenate([conv_x[layer_num], conv_bc[layer_num]], axis=1)
        conv_bias = jnp.concatenate([conv_x_bias[layer_num], conv_bc_bias[layer_num]])
        front_fn = partial(
            mixer_front,
            seg_extended=seg_extended,
            segments=segment_ids,
            head_count=local_heads,
            inner_width=local_inner,
        )
        front_vals, front_back = jax.vjp(
            front_fn,
            extended,
            proj_dt,
            conv_weight,
            conv_bias,
            dt_bias[layer_num],
            a_log[layer_num],
        )
        xs_heads, b_mat, c_mat, step_dt, log_decay = front_vals
        core_fn = partial(mixer_core, segments=segment_ids, block_rows=block_rows)
        core_vals, core_back = jax.vjp(
            core_fn, xs_heads, b_mat, c_mat, step_dt, log_decay, d_skip[layer_num]
        )
        local_y = core_vals[0]
        output_fn = partial(init_output, segments=segment_ids)
        init_y, init_back = jax.vjp(output_fn, log_decay, c_mat, start_state)
        ssd_y = (local_y + init_y).reshape(shard_rows, local_inner)
        gate_vals = jax.nn.silu(proj_z)
        gated_y = ssd_y * gate_vals
        mixed_out = (gated_y * inverse[:, None] * gate_gain[layer_num]).astype(jnp.bfloat16)
        branch_grad = lax.all_gather(grad_hidden.astype(jnp.bfloat16), "tensor", axis=0, tiled=True)
        d_out = jnp.einsum("tk,td->kd", mixed_out, branch_grad, preferred_element_type=jnp.float32)
        d_mixed = jnp.einsum("td,kd->tk", branch_grad, out_full, preferred_element_type=jnp.float32)
        weighted = d_mixed * gate_gain[layer_num]
        inner_dot = lax.psum(jnp.sum(weighted * gated_y, axis=1), "tensor")
        d_gated = (
            inverse[:, None] * weighted
            - gated_y * (inverse * inverse * inverse * inner_dot / full_inner)[:, None]
        )
        d_gate_gain = jnp.sum(d_mixed * gated_y * inverse[:, None], axis=0)
        d_ssd = d_gated * gate_vals
        sigmoid_z = jax.nn.sigmoid(proj_z)
        d_proj_z = (d_gated * ssd_y * sigmoid_z * (1.0 + proj_z * (1.0 - sigmoid_z))).astype(
            jnp.bfloat16
        )
        d_heads = d_ssd.reshape(shard_rows, local_heads, head_width)
        d_decay_first, d_cmat_first, d_start = init_back(d_heads)
        whole_seg = (segment_ids[shard_rows - 1] == segment_ids[0]).astype(jnp.float32)
        coefficient = joined * whole_seg * jnp.exp(jnp.sum(log_decay, axis=0))
        d_end = pass_state(coefficient, joined * d_start, True)
        carry_fn = partial(init_carry, start_state=start_state, segments=segment_ids)
        carry_val, carry_back = jax.vjp(carry_fn, log_decay)
        d_decay_second = carry_back(d_end)[0]
        d_xs, d_bmat, d_cmat_second, d_dt, d_decay_third, d_skip_grad = core_back((d_heads, d_end))
        d_ext, d_proj_dt, d_conv_w, d_conv_b, d_dt_bias, d_log_rate = front_back(
            (
                d_xs,
                d_bmat,
                d_cmat_first + d_cmat_second,
                d_dt,
                d_decay_first + d_decay_second + d_decay_third,
            )
        )
        from_next = passed_along(d_ext[:margin], "dp", -1)
        d_conv_in = d_ext[margin:]
        d_conv_in = jnp.concatenate(
            [d_conv_in[: shard_rows - margin], d_conv_in[shard_rows - margin :] + from_next], axis=0
        )
        d_proj_bc = d_conv_in[:, local_inner:]
        bc_high = d_proj_bc.astype(jnp.bfloat16)
        bc_rest = (d_proj_bc - bc_high.astype(jnp.float32)).astype(jnp.bfloat16)
        zx_width = 2 * local_inner
        state_pair = bc_full.shape[1]
        d_all = jnp.concatenate(
            [
                d_proj_z,
                d_conv_in[:, :local_inner].astype(jnp.bfloat16),
                d_proj_dt.astype(jnp.bfloat16),
                bc_high,
                bc_rest,
            ],
            axis=1,
        )
        w_all = jnp.concatenate(
            [zx_full.reshape(model_width, zx_width), dt_full, bc_full, bc_full], axis=1
        )
        d_weights = jnp.einsum("td,tk->dk", gathered, d_all, preferred_element_type=jnp.float32)
        d_zx = d_weights[:, :zx_width].reshape(model_width, 2, local_inner)
        d_dtw = d_weights[:, zx_width : zx_width + local_heads]
        bc_start = zx_width + local_heads
        d_bcw = (
            d_weights[:, bc_start : bc_start + state_pair] + d_weights[:, bc_start + state_pair :]
        )
        d_normed = lax.psum_scatter(
            jnp.einsum("tk,dk->td", d_all, w_all, preferred_element_type=jnp.float32),
            "tensor",
            scatter_dimension=0,
            tiled=True,
        )
        rms_scale = lax.rsqrt(jnp.mean(hidden_in * hidden_in, axis=1, keepdims=True) + EPSILON)
        gain_grad_in = d_normed * norm_gain[layer_num]
        d_norm_gain = jnp.sum(d_normed * hidden_in * rms_scale, axis=0)
        grad_hidden = (
            grad_hidden
            + rms_scale * gain_grad_in
            - hidden_in
            * rms_scale
            * rms_scale
            * rms_scale
            * jnp.mean(gain_grad_in * hidden_in, axis=1, keepdims=True)
        )
        shards = (
            lax.psum_scatter(d_zx, "dp", scatter_dimension=0, tiled=True),
            lax.psum_scatter(d_dtw, "dp", scatter_dimension=0, tiled=True),
            lax.psum_scatter(d_bcw, "dp", scatter_dimension=0, tiled=True),
            lax.psum_scatter(d_out, "dp", scatter_dimension=1, tiled=True),
        )
        bc_total = lax.psum(shards[2], "tensor")
        totals = lax.psum(
            (
                spread(d_conv_w[:, :local_inner], tensor_rank, tensor_count),
                spread(d_conv_b[:local_inner], tensor_rank, tensor_count),
                d_conv_w[:, local_inner:],
                d_conv_b[local_inner:],
                d_norm_gain,
                spread(d_gate_gain, tensor_rank, tensor_count),
                spread(d_dt_bias, tensor_rank, tensor_count),
                spread(d_log_rate, tensor_rank, tensor_count),
                spread(d_skip_grad, tensor_rank, tensor_count),
            ),
            ("dp", "tensor"),
        )
        layer_results[layer_num] = (shards, totals, (bc_total,))

    def stacked(group, member):
        return jnp.stack([layer_results[layer_num][group][member] for layer_num in range(layers)])

    return (
        y_out,
        grad_hidden,
        stacked(1, 4),
        stacked(0, 0),
        stacked(0, 1),
        stacked(2, 0),
        stacked(1, 0),
        stacked(1, 1),
        stacked(1, 2),
        stacked(1, 3),
        stacked(1, 6),
        stacked(1, 7),
        stacked(1, 8),
        stacked(1, 5),
        stacked(0, 3),
    )


def solution(mesh):
    return jax.shard_map(
        local,
        mesh=mesh,
        in_specs=(
            P(("dp", "tensor"), None),
            P("dp"),
            P(),
            P(None, "dp", None, "tensor"),
            P(None, "dp", "tensor"),
            P(None, "dp", None),
            P(None, None, "tensor"),
            P(None, "tensor"),
            P(),
            P(),
            P(None, "tensor"),
            P(None, "tensor"),
            P(None, "tensor"),
            P(None, "tensor"),
            P(None, "tensor", "dp"),
            P(("dp", "tensor"), None),
        ),
        out_specs=(
            P(("dp", "tensor"), None),
            P(("dp", "tensor"), None),
            P(),
            P(None, "dp", None, "tensor"),
            P(None, "dp", "tensor"),
            P(None, "dp", None),
            P(),
            P(),
            P(),
            P(),
            P(),
            P(),
            P(),
            P(),
            P(None, "tensor", "dp"),
        ),
        check_vma=False,
    )
```

profile of v0, /device:TPU:9, one launch (start us, length us, event | category | flops | bytes accessed | tf_op | source)
XLA Modules:
  0.0 1087.5 jit_solution(12615673510686708438)
XLA Ops:
  24.6 13.7 %all_gather.84 = bf16[256,768]{1,0:T(8,128)(2,1)S(1)} all-gather(bf16[64,768]{1,0:T(8,128)(2,1)S(1)} %fusion.167), channel_id=1, replica_groups=mesh['dp'=8,'tensor'=4] {'tensor'}, dimensions={0}, use_global_device_ids=true | all-gather | bytes 491520 | tf_op jit(solution)/shard_map/all_gather | solution.py:212
  38.3 10.0 all-gather
  54.8 9.3 all-gather.2
  83.6 13.5 %all-gather.5 = bf16[1,384,768]{1,2,0:T(8,128)(2,1)} all-gather(bf16[1,384,96]{1,2,0:T(8,128)(2,1)S(1)} %get-tuple-element.962), channel_id=7, replica_groups=mesh['dp'=8,'tensor'=4] {'dp'}, dimensions={2}, use_global_device_ids=true | all-gather | bytes 663552 | tf_op jit(solution)/shard_map/all_gather | solution.py:202
  100.4 11.4 %all-reduce.26 = f32[48]{0:T(128)S(1)} all-reduce(f32[48]{0:T(128)S(1)} %multiply_dynamic-update-slice_fusion.1), channel_id=6, replica_groups=mesh['dp'=8,'tensor'=4] {'dp'}, use_global_device_ids=true, to_apply=%add.26 | all-reduce | flops 48 | bytes 384
  134.3 18.4 %all-gather.6 = bf16[1,768,6]{2,0,1:T(2,128)(2,1)S(1)} all-gather(bf16[1,96,6]{2,0,1:T(2,128)(2,1)S(1)} %copy.357), channel_id=8, replica_groups=mesh['dp'=8,'tensor'=4] {'dp'}, dimensions={1}, use_global_device_ids=true | all-gather | bytes 10368 | tf_op jit(solution)/shard_map/all_gather | solution.py:200
  153.6 10.2 all-gather.8
  168.3 12.6 %all_gather.92 = bf16[256,768]{1,0:T(8,128)(2,1)S(1)} all-gather(bf16[64,768]{1,0:T(8,128)(2,1)S(1)} %multiply_convert_fusion.10), channel_id=1, replica_groups=mesh['dp'=8,'tensor'=4] {'tensor'}, dimensions={0}, use_global_device_ids=true | all-gather | bytes 491520 | tf_op jit(solution)/shard_map/all_gather | solution.py:212
  201.5 12.5 %all-gather.11 = bf16[1,384,768]{1,2,0:T(8,128)(2,1)} all-gather(bf16[1,384,96]{1,2,0:T(8,128)(2,1)} %get-tuple-element.961), channel_id=13, replica_groups=mesh['dp'=8,'tensor'=4] {'dp'}, dimensions={2}, use_global_device_ids=true | all-gather | bytes 663552 | tf_op jit(solution)/shard_map/all_gather | solution.py:202
  214.0 16.6 %all_gather.100 = bf16[256,768]{1,0:T(8,128)(2,1)} all-gather(bf16[64,768]{1,0:T(8,128)(2,1)} %param.40), channel_id=1, replica_groups=mesh['dp'=8,'tensor'=4] {'tensor'}, dimensions={0}, use_global_device_ids=true | all-gather | bytes 491520 | tf_op jit(solution)/shard_map/all_gather | solution.py:321
  233.0 14.1 %all-reduce.33 = (f32[48]{0:T(128)}, f32[48]{0:T(128)}, f32[48]{0:T(128)}) all-reduce(f32[48]{0:T(128)} %multiply_dynamic-update-slice_fusion, f32[48]{0:T(128)} %multiply_dynamic-update-slice_fusion, f32[48]{0:T(128)} %copy-done.200), channel_id=12, replica_groups=mesh['dp'=8,'tensor'=4] {'dp'}, use_global_device_ids=true, to_apply=%add.27 | all-reduce | flops 144 | bytes 1152
  264.1 8.2 psum.169
  281.8 8.3 psum.170
  315.4 17.2 %all-gather.31.cloned.1.call-done = f32[48,64,128]{2,1,0:T(8,128)} async-done(((f32[6,64,128]{2,1,0:T(8,128)}), f32[48,64,128]{2,1,0:T(8,128)}) %all-gather.31.cloned.1.call-update) | async-done | bytes 1572880 | tf_op jit(solution)/shard_map/all_gather | solution.py:19
  332.6 10.5 while.34
  361.9 8.8 reduce-window.76
  381.4 8.2 reduce-window.96
  418.8 13.6 %reduce-scatter.23.cloned.1.call-done = f32[64,768]{1,0:T(8,128)} async-done(((f32[256,768]{1,0:T(8,128)}), f32[64,768]{1,0:T(8,128)}) %reduce-scatter.23.cloned.1.call-update) | async-done | bytes 196624 | tf_op jit(solution)/shard_map/reduce_scatter | solution.py:384
  435.6 12.5 %all_gather.104 = bf16[256,768]{1,0:T(8,128)(2,1)S(1)} all-gather(bf16[64,768]{1,0:T(8,128)(2,1)S(1)} %fusion.317), channel_id=1, replica_groups=mesh['dp'=8,'tensor'=4] {'tensor'}, dimensions={0}, use_global_device_ids=true | all-gather | bytes 491520 | tf_op jit(solution)/shard_map/all_gather | solution.py:321
  451.5 8.4 psum.171
  481.7 16.4 %all-gather.33.cloned.1.call-done = f32[48,64,128]{2,1,0:T(8,128)} async-done(((f32[6,64,128]{2,1,0:T(8,128)}), f32[48,64,128]{2,1,0:T(8,128)}) %all-gather.33.cloned.1.call-update) | async-done | bytes 1572880 | tf_op jit(solution)/shard_map/all_gather | solution.py:19
  527.4 7.6 reduce-window.102
  567.1 19.3 %reduce-scatter.35.cloned.1.call-done = f32[96,256]{1,0:T(8,128)} async-done(((f32[768,256]{1,0:T(8,128)}), f32[96,256]{1,0:T(8,128)}) %reduce-scatter.35.cloned.1.call-update) | async-done | bytes 98320
  595.4 14.7 %reduce-scatter.25.cloned.1.call-done = f32[64,768]{1,0:T(8,128)} async-done(((f32[256,768]{1,0:T(8,128)}), f32[64,768]{1,0:T(8,128)}) %reduce-scatter.25.cloned.1.call-update) | async-done | bytes 196624 | tf_op jit(solution)/shard_map/reduce_scatter | solution.py:384
  622.2 26.6 %reduce-scatter.33.cloned.1.call-done = f32[96,6]{1,0:T(8,128)} async-done(((f32[768,6]{1,0:T(8,128)}), f32[96,6]{1,0:T(8,128)}) %reduce-scatter.33.cloned.1.call-update) | async-done | bytes 2320
  649.7 39.3 %reduce-scatter.29.cloned.1.call-done = f32[384,96]{0,1:T(8,128)} async-done(((f32[384,768]{0,1:T(8,128)}), f32[384,96]{0,1:T(8,128)}) %reduce-scatter.29.cloned.1.call-update) | async-done | bytes 147472 | tf_op jit(solution)/shard_map/reduce_scatter | solution.py:406
  689.0 39.8 %reduce-scatter.27.cloned.1.call-done = f32[384,96]{0,1:T(8,128)} async-done(((f32[384,768]{0,1:T(8,128)}), f32[384,96]{0,1:T(8,128)}) %reduce-scatter.27.cloned.1.call-update) | async-done | bytes 147472 | tf_op jit(solution)/shard_map/reduce_scatter | solution.py:406
  730.5 34.9 %reduce-scatter.31.cloned.1.call-done = f32[96,6]{1,0:T(8,128)} async-done(((f32[768,6]{1,0:T(8,128)}), f32[96,6]{1,0:T(8,128)}) %reduce-scatter.31.cloned.1.call-update) | async-done | bytes 2320
  766.9 35.6 %all-reduce.44.cloned.1.call-done = (f32[1,96,256]{1,2,0:T(8,128)}, f32[1,96,256]{1,2,0:T(8,128)}) async-done(((f32[1,96,256]{1,2,0:T(8,128)}, f32[1,96,256]{1,2,0:T(8,128)}), (f32[1,96,256]{1,2,0:T(8,128)}, f32[1,96,256]{1,2,0:T(8,128)})) %all-reduce.44.cloned.1.call-update) | async-done | bytes 196624 | tf_op jit(solution)/shard_map/psum | solution.py:408
  804.3 23.1 %reduce-scatter.21.cloned.1.call-done = f32[64,768]{1,0:T(8,128)} async-done(((f32[256,768]{1,0:T(8,128)}), f32[64,768]{1,0:T(8,128)}) %reduce-scatter.21.cloned.1.call-update) | async-done | bytes 196624 | tf_op jit(solution)/shard_map/reduce_scatter | solution.py:253
  829.2 156.1 %all-reduce.40.cloned.1.call-done = (f32[1,768]{1,0:T(1,128)}, f32[1,768]{1,0:T(1,128)}, f32[1,4,1536]{2,1,0:T(4,128)}, f32[1,4,1536]{2,1,0:T(4,128)}, f32[1,153...) async-done(((f32[1,768]{1,0:T(1,128)}, f32[1,768]{1,0:T(1,128)}, ...) | async-done | bytes 90704 | tf_op jit(solution)/shard_map/psum | solution.py:409
  996.8 80.7 %all-reduce.42.cloned.1.call-done = (f32[768,2,384]{2,1,0:T(2,128)}, f32[768,2,384]{2,1,0:T(2,128)}) async-done(((f32[768,2,384]{2,1,0:T(2,128)}, f32[768,2,384]{2,1,0:T(2,128)}), (f32[768,2,384]{2,1,0:T(2,128)}, f32[768,2,384]{2,1,0:T(2,128)})) %all-reduce.42.cloned.1.call-update) | async-done | bytes 4718608
  (819 shorter events, 352.8 us)
Async XLA Ops:
  7.2 60.8 %all-gather.23.cloned.1.call-start = ((), (), s32[]{:S(2)}) async-start(), calls=%async_computation.16 | async-start | bytes 1327104 | tf_op jit(solution)/shard_map/all_gather | solution.py:199
  8.0 57.9 %collective-permute-start.1 = (bf16[3]{0:T(256)(128)(2,1)S(1)}, bf16[3]{0:T(256)(128)(2,1)S(1)}, u32[]{:S(2)}, u32[]{:S(2)}) collective-permute-start(bf16[3]{0:T(256)(128)(2,1)S(1)} %add_convert_fusion.1), channel_id=1, source_target_pairs={{0,4},{4,8},{8,12},{12,16},{16,20},{20,24},{24,28},{1,5},{5,9},{9,... | collective-permute-start | bytes 26 | tf_op jit(solution)/shard_map/ppermute | solution.py:34
  13.8 101.0 %all-gather.25.cloned.1.call-start = ((), (), s32[]{:S(2)}) async-start(), calls=%async_computation.17 | async-start | bytes 1769472 | tf_op jit(solution)/shard_map/all_gather | solution.py:19
  70.1 3.2 collective-permute-start
  78.0 86.5 %all-gather.27.cloned.1.call-start = ((), (), s32[]{:S(2)}) async-start(), calls=%async_computation.18 | async-start | bytes 1327104 | tf_op jit(solution)/shard_map/all_gather | solution.py:199
  78.7 88.3 %reduce-scatter.19.cloned.1.call-start = ((), (), s32[]{:S(2)}) async-start(), calls=%async_computation.10 | async-start | bytes 983040 | tf_op jit(solution)/shard_map/reduce_scatter | solution.py:253
  134.1 118.6 %all-gather.29.cloned.1.call-start = ((), (), s32[]{:S(2)}) async-start(), calls=%async_computation.19 | async-start | bytes 1769472 | tf_op jit(solution)/shard_map/all_gather | solution.py:19
  189.8 5.0 collective-permute-start.2
  199.2 53.5 %copy-start.33 = (f32[256,384]{0,1:T(8,128)}, f32[256,384]{0,1:T(8,128)S(1)}, u32[]{:S(2)}) copy-start(f32[256,384]{0,1:T(8,128)S(1)} %copy.293) | copy-start | bytes 1179652
  201.5 131.1 %all-gather.31.cloned.1.call-start = ((), (), s32[]{:S(2)}) async-start(), calls=%async_computation.20 | async-start | bytes 1769472 | tf_op jit(solution)/shard_map/all_gather | solution.py:19
  297.4 135.0 %reduce-scatter.23.cloned.1.call-start = ((), (), s32[]{:S(2)}) async-start(), calls=%async_computation.12 | async-start | bytes 983040 | tf_op jit(solution)/shard_map/reduce_scatter | solution.py:384
  397.8 8.2 collective-permute-start.3
  412.7 85.3 %all-gather.33.cloned.1.call-start = ((), (), s32[]{:S(2)}) async-start(), calls=%async_computation.21 | async-start | bytes 1769472 | tf_op jit(solution)/shard_map/all_gather | solution.py:19
  412.8 94.9 %copy-start.118 = (f32[1,6,2,128]{3,1,2,0:T(8,128)}, f32[1,6,2,128]{3,1,2,0:T(8,128)S(1)}, u32[]{:S(2)}) copy-start(f32[1,6,2,128]{3,1,2,0:T(8,128)S(1)} %copy.439) | copy-start | bytes 18436
  467.0 98.4 %reduce-scatter.37.cloned.1.call-start = ((), (), s32[]{:S(2)}) async-start(), calls=%async_computation.25 | async-start | bytes 884736
  474.3 112.1 %reduce-scatter.35.cloned.1.call-start = ((), (), s32[]{:S(2)}) async-start(), calls=%async_computation.24 | async-start | bytes 884736
  537.9 7.3 collective-permute-start.4
  553.2 56.9 %reduce-scatter.25.cloned.1.call-start = ((), (), s32[]{:S(2)}) async-start(), calls=%async_computation.13 | async-start | bytes 983040 | tf_op jit(solution)/shard_map/reduce_scatter | solution.py:384
  560.0 88.9 %reduce-scatter.33.cloned.1.call-start = ((), (), s32[]{:S(2)}) async-start(), calls=%async_computation.23 | async-start | bytes 442368
  561.0 128.0 %reduce-scatter.29.cloned.1.call-start = ((), (), s32[]{:S(2)}) async-start(), calls=%async_computation.15 | async-start | bytes 1327104 | tf_op jit(solution)/shard_map/reduce_scatter | solution.py:406
  562.7 166.1 %reduce-scatter.27.cloned.1.call-start = ((), (), s32[]{:S(2)}) async-start(), calls=%async_computation.14 | async-start | bytes 1327104 | tf_op jit(solution)/shard_map/reduce_scatter | solution.py:406
  564.3 201.2 %reduce-scatter.31.cloned.1.call-start = ((), (), s32[]{:S(2)}) async-start(), calls=%async_computation.22 | async-start | bytes 442368
  565.3 237.2 %all-reduce.44.cloned.1.call-start = ((), (), s32[]{:S(2)}) async-start(), calls=%async_computation.28 | async-start | bytes 524288 | tf_op jit(solution)/shard_map/psum | solution.py:408
  588.3 239.1 %reduce-scatter.21.cloned.1.call-start = ((), (), s32[]{:S(2)}) async-start(), calls=%async_computation.11 | async-start | bytes 983040 | tf_op jit(solution)/shard_map/reduce_scatter | solution.py:253
  590.0 395.3 %all-reduce.40.cloned.1.call-start = ((), (), s32[]{:S(2)}) async-start(), calls=%async_computation.26 | async-start | bytes 186368 | tf_op jit(solution)/shard_map/psum | solution.py:409
  612.0 465.5 %all-reduce.42.cloned.1.call-start = ((), (), s32[]{:S(2)}) async-start(), calls=%async_computation.27 | async-start | bytes 9437184
  621.5 205.9 %copy-start.23 = (f32[64,768]{1,0:T(8,128)S(1)}, f32[64,768]{1,0:T(8,128)}, u32[]{:S(2)}) copy-start(f32[64,768]{1,0:T(8,128)} %copy-done.21) | copy-start | bytes 589828
  621.5 205.9 %copy-start.38 = (f32[64,768]{1,0:T(8,128)S(1)}, f32[64,768]{1,0:T(8,128)}, u32[]{:S(2)}) copy-start(f32[64,768]{1,0:T(8,128)} %reduce-scatter.23.cloned.1.call-done) | copy-start | bytes 589828
  621.5 205.9 %copy-start.50 = (bf16[64,768]{1,0:T(8,128)(2,1)S(1)}, bf16[64,768]{1,0:T(8,128)(2,1)}, u32[]{:S(2)}) copy-start(bf16[64,768]{1,0:T(8,128)(2,1)} %param.40) | copy-start | bytes 294916
  621.5 205.8 %copy-start.51 = (f32[64,768]{1,0:T(8,128)S(1)}, f32[64,768]{1,0:T(8,128)}, u32[]{:S(2)}) copy-start(f32[64,768]{1,0:T(8,128)} %reduce-scatter.25.cloned.1.call-done) | copy-start | bytes 589828
  621.5 205.8 %copy-start.147 = (f32[64]{0:T(128)S(1)}, f32[64]{0:T(128)}, u32[]{:S(2)}) copy-start(f32[64]{0:T(128)} %copy-done.145) | copy-start | bytes 772
  621.5 205.8 %copy-start.177 = (f32[64]{0:T(128)S(1)}, f32[64]{0:T(128)}, u32[]{:S(2)}) copy-start(f32[64]{0:T(128)} %copy-done.176) | copy-start | bytes 772
  (197 other events, 2036.3 us)
Sparse Core Ops, SparseCore 0:
  13.9 24.0 all-gather.22
  78.1 28.6 all-gather.24
  109.2 23.9 all-gather.26
  135.4 29.2 reduce-scatter.18
  201.6 28.0 all-gather.28
  297.5 35.0 all-gather.30
  412.8 19.5 reduce-scatter.22
  467.1 30.8 all-gather.32
  501.2 34.0 reduce-scatter.36
  553.3 33.0 reduce-scatter.34
  588.7 21.3 reduce-scatter.24
  613.6 35.2 reduce-scatter.32
  652.1 36.8 reduce-scatter.28
  692.1 36.6 reduce-scatter.26
  731.7 33.6 reduce-scatter.30
  768.2 34.1 all-reduce.43
  804.6 22.6 reduce-scatter.20
  834.8 150.4 all-reduce.39
  988.6 88.7 all-reduce.41
where the time goes:
time: 1100 us; the launch traced here: 1090 us
  waiting for transfers between devices  518 us (47%)
  blocking collectives  187 us (17%)
  other arithmetic  129 us (12%)
  local copies, waits for them, and re-layouts  116 us (11%)
  matrix products  94.3 us (9%)
  between operations  22.7 us (2%)
  starting transfers between devices  19.1 us (2%)
    unnamed x24, waiting for transfers between devices  162 us
    psum x1, waiting for transfers between devices, local(): lax.psum((spread(d_conv_w[:, :local_inner], tensor_rank, tensor_count), s...  156 us
    reduce_scatter x2, waiting for transfers between devices, local(): lax.psum_scatter(d_out, 'dp', scatter_dimension=1, tiled=True)  79.1 us
    another operation x22, other arithmetic  46 us
    psum x1, waiting for transfers between devices, local(): bc_total = lax.psum(shards[2], 'tensor')  35.6 us
    all_gather x4, waiting for transfers between devices, entering(): gathered = jax.tree.map(lambda a: lax.all_gather(a, axis), part)  33.6 us
    dot_general x8, matrix products, stretch_core(): jnp.einsum('ijh,ij,jhp->ihp', decays, scores, scaled, precision=PRECISE)  33.2 us
    unnamed x424, local copies, waits for them, and re-layouts  32.4 us
  transfers between devices with their start and end apart: 24, of which 14 were waited for; matrix products, arithmetic and copies ran while one was open for 17% of the time, Pallas kernels for 0%

commit v1 on v0

v1 whole, which is shorter than its diff:
```python
import jax
import jax.numpy as jnp
from jax import lax
from jax.experimental import pallas as pl
from jax.experimental.pallas import tpu as pltpu
from jax.sharding import PartitionSpec as P

EPSILON = 1e-05
PRECISE = lax.Precision.HIGHEST
CORE = lax.Precision.HIGH
MESH = pl.DeviceIdType.MESH


def exchange(parts, axis, collective_id):
    count = lax.axis_size(axis)
    many = len(parts)
    block_shapes = [a.shape[1:] if scatter else a.shape for a, scatter, _ in parts]
    outs, slots = [], []
    for (a, _, reduce), shape in zip(parts, block_shapes):
        if reduce:
            outs.append(jax.ShapeDtypeStruct(shape, jnp.float32))
            slots.append(pltpu.VMEM((count,) + shape, a.dtype))
        else:
            outs.append(jax.ShapeDtypeStruct((count,) + shape, a.dtype))

    def kernel(*refs):
        ins, results = refs[:many], refs[many : 2 * many]
        scratch = list(refs[2 * many : len(refs) - 3])
        send_sem, recv_sem, own_sem = refs[len(refs) - 3 :]
        landing = [
            scratch.pop(0) if reduce else results[i] for i, (_, _, reduce) in enumerate(parts)
        ]
        me = lax.axis_index(axis)
        barrier = pltpu.get_barrier_semaphore()
        for step in range(1, count):
            peer = lax.rem(me + step, count)
            pl.semaphore_signal(barrier, inc=1, device_id={axis: peer}, device_id_type=MESH)
        own = []
        for i, (_, scatter, _) in enumerate(parts):
            block = ins[i].at[me] if scatter else ins[i]
            copy = pltpu.make_async_copy(block, landing[i].at[me], own_sem.at[i])
            copy.start()
            own.append(copy)
        pl.semaphore_wait(barrier, count - 1)
        sent = []
        for step in range(1, count):
            peer = lax.rem(me + step, count)
            for i, (_, scatter, _) in enumerate(parts):
                copy = pltpu.make_async_remote_copy(
                    src_ref=ins[i].at[peer] if scatter else ins[i],
                    dst_ref=landing[i].at[me],
                    send_sem=send_sem.at[i, step - 1],
                    recv_sem=recv_sem.at[i, step - 1],
                    device_id={axis: peer},
                    device_id_type=MESH,
                )
                copy.start()
                sent.append(copy)
        for copy in own:
            copy.wait()
        for copy in sent:
            copy.wait()
        for i, (_, _, reduce) in enumerate(parts):
            if reduce:
                total = landing[i][0].astype(jnp.float32)
                for source in range(1, count):
                    total = total + landing[i][source].astype(jnp.float32)
                results[i][...] = total

    return pl.pallas_call(
        kernel,
        out_shape=tuple(outs),
        in_specs=[pl.BlockSpec(memory_space=pltpu.VMEM)] * many,
        out_specs=tuple([pl.BlockSpec(memory_space=pltpu.VMEM)] * many),
        scratch_shapes=slots
        + [
            pltpu.SemaphoreType.DMA((many, count - 1)),
            pltpu.SemaphoreType.DMA((many, count - 1)),
            pltpu.SemaphoreType.DMA((many,)),
        ],
        compiler_params=pltpu.CompilerParams(collective_id=collective_id, has_side_effects=True),
    )(*[a for a, _, _ in parts])


def rows_from_all(rows, collective_id):
    (out,) = exchange([(rows, False, False)], "tensor", collective_id)
    return out.reshape(-1, rows.shape[1])


def rows_summed(partial_rows, collective_id):
    count = lax.axis_size("tensor")
    blocks = partial_rows.astype(jnp.bfloat16).reshape(count, -1, partial_rows.shape[1])
    return exchange([(blocks, True, True)], "tensor", collective_id)[0]


def token_sums(values, collective_id):
    length = values.shape[0]
    return exchange([(values.reshape(-1, 128), False, True)], "tensor", collective_id)[0].reshape(
        length
    )


def passed_along(block, axis, distance):
    devices = range(lax.axis_size(axis))
    route = [(i - distance, i) for i in devices if i - distance in devices]
    return lax.ppermute(block, axis, route)


def entering(coefficients, values, backward):
    count = values.shape[0]
    place = lax.axis_index("dp")
    state = jnp.zeros(values.shape[1:], jnp.float32)
    for source in reversed(range(count)) if backward else range(count):
        ahead = source > place if backward else source < place
        later = values[source].astype(jnp.float32) + coefficients[source][:, None, None] * state
        state = jnp.where(ahead, later, state)
    return state


def mixer_core(xs_heads, b_mat, c_mat, step_dt, log_decay, skip_gain, segments):
    length = segments.shape[0]
    places = jnp.arange(length)
    below = places[:, None] >= places[None, :]
    cumulative = jnp.dot(below.astype(jnp.float32), log_decay, precision=PRECISE)
    inside = (segments[:, None] == segments[None, :]) & below
    by_head = cumulative.T
    span_logs = by_head[:, :, None] - by_head[:, None, :]
    decays = jnp.exp(jnp.where(inside[None], span_logs, -1e30))
    scores = jnp.dot(c_mat, b_mat.T, precision=CORE)
    scaled = xs_heads * step_dt[:, :, None]
    output = jnp.einsum("hij,jhp->ihp", decays * scores[None], scaled, precision=CORE)
    output = output + skip_gain[None, :, None] * xs_heads
    kept_rows = (segments == segments[length - 1]).astype(jnp.float32)
    to_end = jnp.exp(cumulative[length - 1][None, :] - cumulative) * kept_rows[:, None]
    state = jnp.einsum("jhp,jn->hpn", scaled * to_end[:, :, None], b_mat, precision=CORE)
    return (output, state, cumulative)


def init_output(cumulative, c_mat, start_state, segments):
    reached = (segments == segments[0]).astype(jnp.float32)
    carried = jnp.einsum("tn,hpn->thp", c_mat, start_state, precision=CORE)
    return (jnp.exp(cumulative) * reached[:, None])[:, :, None] * carried


def conv_apply(extended, seg_extended, segments, conv_weight, conv_bias):
    length = segments.shape[0]
    tap_count = conv_weight.shape[0]
    result = jnp.zeros((length, extended.shape[1]), jnp.float32) + conv_bias
    for tap_index in range(tap_count):
        same_seg = (seg_extended[tap_index : tap_index + length] == segments).astype(jnp.float32)
        result = (
            result
            + conv_weight[tap_index] * extended[tap_index : tap_index + length] * same_seg[:, None]
        )
    return result


def mixer_front(
    extended,
    proj_dt,
    conv_weight,
    conv_bias,
    bias_dt,
    log_rate,
    seg_extended,
    segments,
    head_count,
    inner_width,
):
    activated = jax.nn.silu(conv_apply(extended, seg_extended, segments, conv_weight, conv_bias))
    length = segments.shape[0]
    state_width = (activated.shape[1] - inner_width) // 2
    xs_heads = activated[:, :inner_width].reshape(length, head_count, inner_width // head_count)
    b_mat = activated[:, inner_width : inner_width + state_width]
    c_mat = activated[:, inner_width + state_width :]
    step_dt = jax.nn.softplus(proj_dt + bias_dt)
    log_decay = -step_dt * jnp.exp(log_rate)
    return (xs_heads, b_mat, c_mat, step_dt, log_decay)


def local(
    x_in,
    segment_ids,
    norm_gain,
    w_zx,
    w_dt,
    w_bc,
    conv_x,
    conv_x_bias,
    conv_bc,
    conv_bc_bias,
    dt_bias,
    a_log,
    d_skip,
    gate_gain,
    w_out,
    cotangent,
):
    layers = norm_gain.shape[0]
    tensor_count = lax.axis_size("tensor")
    data_count = lax.axis_size("dp")
    model_width = x_in.shape[1]
    shard_rows = segment_ids.shape[0]
    local_inner = conv_x.shape[2]
    local_heads = dt_bias.shape[1]
    state_pair = w_bc.shape[2]
    state_width = state_pair // 2
    head_width = local_inner // local_heads
    full_inner = local_inner * tensor_count
    margin = conv_x.shape[1] - 1
    dt_room = -local_heads % 128 + local_heads
    at_bc = 2 * local_inner
    at_dt = at_bc + state_pair
    at_out = at_dt + dt_room
    width = at_out + local_inner
    ids = iter(range(1, 64))

    packed = [
        jnp.concatenate(
            [
                w_zx[l].reshape(-1, at_bc),
                w_bc[l],
                jnp.pad(w_dt[l], ((0, 0), (0, dt_room - local_heads))),
                w_out[l].T,
            ],
            axis=1,
        )
        for l in range(layers)
    ]
    weights_all = []
    for l in range(layers):
        if l == 0:
            (full,) = exchange([(packed[l], False, False)], "dp", next(ids))
            weights_all.append(full.reshape(model_width, width))
        else:
            weights_all.append(lax.all_gather(packed[l], "dp", axis=0, tiled=True))

    seg_tail = (segment_ids[shard_rows - margin :] + 1).astype(jnp.bfloat16)
    tail_segs = passed_along(seg_tail, "dp", 1)
    seg_extended = jnp.concatenate([tail_segs.astype(jnp.int32) - 1, segment_ids])
    joined = (seg_extended[margin - 1] == segment_ids[0]).astype(jnp.float32)
    whole_seg = (segment_ids[shard_rows - 1] == segment_ids[0]).astype(jnp.float32)

    hidden = x_in.astype(jnp.float32)
    records = []
    for layer_num in range(layers):
        weights = weights_all[layer_num]
        rms_scale = lax.rsqrt(jnp.mean(hidden * hidden, axis=1, keepdims=True) + EPSILON)
        normed = (hidden * rms_scale * norm_gain[layer_num]).astype(jnp.bfloat16)
        gathered = rows_from_all(normed, next(ids))
        projected = jnp.dot(gathered, weights[:, :at_out], preferred_element_type=jnp.float32)
        proj_z = projected[:, :local_inner]
        proj_dt = projected[:, at_dt : at_dt + local_heads]
        conv_in = projected[:, local_inner:at_dt].astype(jnp.bfloat16)
        tail_rows = passed_along(conv_in[shard_rows - margin :], "dp", 1)
        extended = jnp.concatenate([tail_rows, conv_in], axis=0).astype(jnp.float32)
        conv_weight = jnp.concatenate([conv_x[layer_num], conv_bc[layer_num]], axis=1)
        conv_bias = jnp.concatenate([conv_x_bias[layer_num], conv_bc_bias[layer_num]])

        def front_fn(extended, proj_dt, conv_weight, conv_bias, bias_dt, log_rate):
            return mixer_front(
                extended,
                proj_dt,
                conv_weight,
                conv_bias,
                bias_dt,
                log_rate,
                seg_extended,
                segment_ids,
                local_heads,
                local_inner,
            )

        front_vals, front_back = jax.vjp(
            front_fn,
            extended,
            proj_dt,
            conv_weight,
            conv_bias,
            dt_bias[layer_num],
            a_log[layer_num],
        )
        xs_heads, b_mat, c_mat, step_dt, log_decay = front_vals
        core_vals, core_back = jax.vjp(
            lambda *args: mixer_core(*args, segment_ids),
            xs_heads,
            b_mat,
            c_mat,
            step_dt,
            log_decay,
            d_skip[layer_num],
        )
        local_y, local_state, cumulative = core_vals
        end_decay = jnp.exp(cumulative[shard_rows - 1])
        coefficient = joined * whole_seg * end_decay
        coefficients, states = exchange(
            [
                (jnp.pad(coefficient, (0, dt_room - local_heads)).reshape(-1, 128), False, False),
                (
                    local_state.astype(jnp.bfloat16).reshape(local_inner, state_width),
                    False,
                    False,
                ),
            ],
            "dp",
            next(ids),
        )
        coefficients = coefficients.reshape(data_count, dt_room)[:, :local_heads]
        states = states.reshape(data_count, local_heads, head_width, state_width)
        start_state = joined * entering(coefficients, states, False)
        init_y, init_back = jax.vjp(
            lambda *args: init_output(*args, segment_ids), cumulative, c_mat, start_state
        )
        ssd_y = (local_y + init_y).reshape(shard_rows, local_inner)
        gate_vals = jax.nn.silu(proj_z)
        gated_y = ssd_y * gate_vals
        squares = token_sums(jnp.sum(gated_y * gated_y, axis=1), next(ids))
        inverse = lax.rsqrt(squares / full_inner + EPSILON)
        mixed_out = (gated_y * inverse[:, None] * gate_gain[layer_num]).astype(jnp.bfloat16)
        branch = rows_summed(
            jnp.einsum(
                "tk,dk->td",
                mixed_out,
                weights[:, at_out:],
                preferred_element_type=jnp.float32,
            ),
            next(ids),
        )
        records.append(
            (
                hidden,
                gathered,
                proj_z,
                ssd_y,
                gate_vals,
                gated_y,
                mixed_out,
                inverse,
                start_state,
                end_decay,
                coefficients,
                front_back,
                core_back,
                init_back,
            )
        )
        hidden = hidden + branch
    y_out = hidden.astype(jnp.bfloat16)
    grad_hidden = cotangent.astype(jnp.float32)
    weight_grads = [None] * layers
    small_grads = [None] * layers
    for layer_num in reversed(range(layers)):
        (
            hidden_in,
            gathered,
            proj_z,
            ssd_y,
            gate_vals,
            gated_y,
            mixed_out,
            inverse,
            start_state,
            end_decay,
            coefficients,
            front_back,
            core_back,
            init_back,
        ) = records[layer_num]
        weights = weights_all[layer_num]
        branch_grad = rows_from_all(grad_hidden.astype(jnp.bfloat16), next(ids))
        d_out = jnp.einsum("td,tk->dk", branch_grad, mixed_out, preferred_element_type=jnp.float32)
        d_mixed = jnp.einsum(
            "td,dk->tk", branch_grad, weights[:, at_out:], preferred_element_type=jnp.float32
        )
        weighted = d_mixed * gate_gain[layer_num]
        inner_dot = token_sums(jnp.sum(weighted * gated_y, axis=1), next(ids))
        d_gated = (
            inverse[:, None] * weighted
            - gated_y * (inverse * inverse * inverse * inner_dot / full_inner)[:, None]
        )
        d_gate_gain = jnp.sum(d_mixed * gated_y * inverse[:, None], axis=0)
        d_ssd = d_gated * gate_vals
        sigmoid_z = jax.nn.sigmoid(proj_z)
        d_proj_z = (d_gated * ssd_y * sigmoid_z * (1.0 + proj_z * (1.0 - sigmoid_z))).astype(
            jnp.bfloat16
        )
        d_heads = d_ssd.reshape(shard_rows, local_heads, head_width)
        d_cum, d_cmat_first, d_start = init_back(d_heads)
        (d_states,) = exchange(
            [
                (
                    (joined * d_start).astype(jnp.bfloat16).reshape(local_inner, state_width),
                    False,
                    False,
                )
            ],
            "dp",
            next(ids),
        )
        d_end = entering(
            coefficients,
            d_states.reshape(data_count, local_heads, head_width, state_width),
            True,
        )
        d_last = whole_seg * end_decay * jnp.sum(d_end * start_state, axis=(1, 2))
        d_cum = d_cum + jnp.where(
            jnp.arange(shard_rows)[:, None] == shard_rows - 1, d_last[None, :], 0.0
        )
        d_xs, d_bmat, d_cmat_second, d_dt, d_decay, d_skip_grad = core_back((d_heads, d_end, d_cum))
        d_ext, d_proj_dt, d_conv_w, d_conv_b, d_dt_bias, d_log_rate = front_back(
            (d_xs, d_bmat, d_cmat_first + d_cmat_second, d_dt, d_decay)
        )
        from_next = passed_along(d_ext[:margin], "dp", -1)
        d_conv_in = d_ext[margin:]
        d_conv_in = jnp.concatenate(
            [d_conv_in[: shard_rows - margin], d_conv_in[shard_rows - margin :] + from_next], axis=0
        )
        d_proj_bc = d_conv_in[:, local_inner:]
        bc_high = d_proj_bc.astype(jnp.bfloat16)
        bc_rest = (d_proj_bc - bc_high.astype(jnp.float32)).astype(jnp.bfloat16)
        d_all = jnp.concatenate(
            [
                d_proj_z,
                d_conv_in[:, :local_inner].astype(jnp.bfloat16),
                bc_high,
                jnp.pad(
                    d_proj_dt.astype(jnp.bfloat16), ((0, 0), (0, dt_room - local_heads))
                ),
            ],
            axis=1,
        )
        d_normed = rows_summed(
            jnp.einsum(
                "tk,dk->td", d_all, weights[:, :at_out], preferred_element_type=jnp.float32
            )
            + jnp.einsum(
                "tk,dk->td", bc_rest, weights[:, at_bc:at_dt], preferred_element_type=jnp.float32
            ),
            next(ids),
        )
        d_in = jnp.einsum("td,tk->dk", gathered, d_all, preferred_element_type=jnp.float32)
        d_rest = jnp.einsum("td,tk->dk", gathered, bc_rest, preferred_element_type=jnp.float32)
        weight_grads[layer_num] = jnp.concatenate(
            [
                d_in[:, :at_bc].astype(jnp.bfloat16),
                (d_in[:, at_bc:at_dt] + d_rest).astype(jnp.bfloat16),
                d_in[:, at_dt:].astype(jnp.bfloat16),
                d_out.astype(jnp.bfloat16),
            ],
            axis=1,
        ).reshape(data_count, model_width // data_count, width)
        rms_scale = lax.rsqrt(jnp.mean(hidden_in * hidden_in, axis=1, keepdims=True) + EPSILON)
        gain_grad_in = d_normed * norm_gain[layer_num]
        d_norm_gain = jnp.sum(d_normed * hidden_in * rms_scale, axis=0)
        grad_hidden = (
            grad_hidden
            + rms_scale * gain_grad_in
            - hidden_in
            * rms_scale
            * rms_scale
            * rms_scale
            * jnp.mean(gain_grad_in * hidden_in, axis=1, keepdims=True)
        )
        small_grads[layer_num] = (
            d_conv_w[:, :local_inner],
            d_conv_b[:local_inner],
            d_gate_gain,
            d_dt_bias,
            d_log_rate,
            d_skip_grad,
            d_conv_w[:, local_inner:],
            d_conv_b[local_inner:],
            d_norm_gain,
        )

    small = [jnp.stack([small_grads[l][m] for l in range(layers)]) for m in range(9)]
    flat = jnp.concatenate([s.reshape(-1) for s in small])
    flat = jnp.pad(flat, (0, -flat.shape[0] % 1024)).reshape(-1, 128)
    reduced = exchange(
        [(g, True, True) for g in weight_grads] + [(flat, False, True)], "dp", next(ids)
    )
    grads, flat = jnp.stack(reduced[:layers]), reduced[layers]
    d_bc = grads[:, :, at_bc:at_dt].astype(jnp.bfloat16)
    flats, bc_total = exchange(
        [(flat, False, False), (d_bc, False, True)], "tensor", next(ids)
    )
    flats = flats.reshape(tensor_count, -1)
    totals, start = [], 0
    for m, s in enumerate(small):
        piece = flats[:, start : start + s.size].reshape((tensor_count,) + s.shape)
        start += s.size
        if m < 6:
            joined_up = jnp.moveaxis(piece, 0, -2)
            totals.append(joined_up.reshape(s.shape[:-1] + (tensor_count * s.shape[-1],)))
        else:
            totals.append(jnp.sum(piece, axis=0))
    return (
        y_out,
        grad_hidden,
        totals[8],
        grads[:, :, :at_bc].reshape(layers, -1, 2, local_inner),
        grads[:, :, at_dt : at_dt + local_heads],
        bc_total,
        totals[0],
        totals[1],
        totals[6],
        totals[7],
        totals[3],
        totals[4],
        totals[5],
        totals[2],
        jnp.swapaxes(grads[:, :, at_out:], 1, 2),
    )


def solution(mesh):
    return jax.shard_map(
        local,
        mesh=mesh,
        in_specs=(
            P(("dp", "tensor"), None),
            P("dp"),
            P(),
            P(None, "dp", None, "tensor"),
            P(None, "dp", "tensor"),
            P(None, "dp", None),
            P(None, None, "tensor"),
            P(None, "tensor"),
            P(),
            P(),
            P(None, "tensor"),
            P(None, "tensor"),
            P(None, "tensor"),
            P(None, "tensor"),
            P(None, "tensor", "dp"),
            P(("dp", "tensor"), None),
        ),
        out_specs=(
            P(("dp", "tensor"), None),
            P(("dp", "tensor"), None),
            P(),
            P(None, "dp", None, "tensor"),
            P(None, "dp", "tensor"),
            P(None, "dp", None),
            P(),
            P(),
            P(),
            P(),
            P(),
            P(),
            P(),
            P(),
            P(None, "tensor", "dp"),
        ),
        check_vma=False,
    )
```

time: 1100 us -> 552 us (0.50)
  waiting for transfers between devices: 518 us -> 0.03 us
  Pallas kernels: 0 us -> 296 us
  blocking collectives: 187 us -> 0 us
  other arithmetic: 129 us -> 66 us
  matrix products: 94.3 us -> 52.3 us
  local copies, waits for them, and re-layouts: 116 us -> 93.5 us
    pallas_call x0 -> x19, Pallas kernels: none -> 296 us  [exchange(): pl.pallas_call(kernel, out_shape=tuple(outs), in_specs=[pl.BlockSpec(memo...]
    psum x2 -> x0, waiting for transfers between devices: 192 us -> none  [the longest x1 156 us: local(): lax.psum((spread(d_conv_w[:, :local_inner], tensor_rank, tensor_count), s...]
    unnamed x24 -> x1, waiting for transfers between devices: 162 us -> 0.02 us
    reduce_scatter x6 -> x0, waiting for transfers between devices: 131 us -> none  [the longest x2 79.1 us: local(): lax.psum_scatter(d_out, 'dp', scatter_dimension=1, tiled=True)]
    all_gather x10 -> x0, blocking collectives: 129 us -> none  [the longest x2 29.1 us: local(): lax.all_gather(grad_hidden.astype(jnp.bfloat16), 'tensor', axis=0, tiled=...]
    another operation x38 -> x14, other arithmetic: 62.5 us -> 2.63 us  [the longest x9 1.86 us: local(): jnp.stack([small_grads[l][m] for l in range(layers)])]
    dot_general x44 -> x42, matrix products: 91.7 us -> 50.8 us  [the longest x6 13.5 us: mixer_core(): jnp.einsum('hij,jhp->ihp', decays * scores[None], scaled, precision=CORE)]
    all_gather x6 -> x1, waiting for transfers between devices: 33.6 us -> 0.01 us  [local(): weights_all.append(lax.all_gather(packed[l], 'dp', axis=0, tiled=True))]
  transfers between devices with their start and end apart: 24 -> 6, of which waited for: 14 -> 0; matrix products, arithmetic and copies ran while one was open for 17% -> 15% of each run, Pallas kernels for 0% -> 13%
where the time goes in v1:
time: 552 us; the launch traced here: 541 us
  Pallas kernels  296 us (54%)
  local copies, waits for them, and re-layouts  93.5 us (17%)
  other arithmetic  66 us (12%)
  matrix products  52.3 us (9%)
  between operations  20.4 us (4%)
  starting transfers between devices  12.4 us (2%)
    pallas_call x19, Pallas kernels, exchange(): pl.pallas_call(kernel, out_shape=tuple(outs), in_specs=[pl.BlockSpec(memo...  296 us
    mul x42, local copies, waits for them, and re-layouts, entering(): coefficients[source][:, None, None] * state  16.9 us
    unnamed x468, local copies, waits for them, and re-layouts  14.2 us
    dot_general x6, matrix products, mixer_core(): jnp.einsum('hij,jhp->ihp', decays * scores[None], scaled, precision=CORE)  13.5 us
    ppermute x5, starting transfers between devices, passed_along(): return lax.ppermute(block, axis, route)  12.4 us
  transfers between devices with their start and end apart: 6, of which 0 were waited for; matrix products, arithmetic and copies ran while one was open for 15% of the time, Pallas kernels for 13%

profile of v1, /device:TPU:9, one launch (start us, length us, event | category | flops | bytes accessed | tf_op | source)
XLA Modules:
  0.0 540.9 jit_solution(1096828462510808472)
XLA Ops:
  11.9 31.8 %shard_map.272 = bf16[8,96,1536]{2,1,0:T(8,128)(2,1)} custom-call(bf16[96,1536]{1,0:T(8,128)(2,1)} %fusion.131.refs_0_), custom_call_target="tpu_custom_call" | custom-call | tf_op jit(solution)/shard_map/pallas_call | solution.py:70
  44.6 13.9 %shard_map.271 = bf16[4,64,768]{2,1,0:T(8,128)(2,1)} custom-call(bf16[64,768]{1,0:T(8,128)(2,1)} %fusion.142.refs_0_), custom_call_target="tpu_custom_call" | custom-call | tf_op jit(solution)/shard_map/pallas_call | solution.py:70
  60.9 2.6 collective-permute-start
  70.4 13.4 %shard_map.280 = bf16[4,64,768]{2,1,0:T(8,128)(2,1)} custom-call(bf16[64,768]{1,0:T(8,128)(2,1)} %refs_0_), custom_call_target="tpu_custom_call" | custom-call | tf_op jit(solution)/shard_map/pallas_call | solution.py:70
  96.0 14.4 %shard_map.273 = (f32[8,1,128]{2,1,0:T(1,128)}, bf16[8,384,128]{2,1,0:T(8,128)(2,1)}) custom-call(f32[1,128]{1,0:T(1,128)} %pad_bitcast_fusion.2.refs_0_, bf16[384,128]{1,0:T(8,128)(2,1)} %bitcast.434), custom_call_target="tpu_custom_call" | custom-call | tf_op jit(solution)/shard_map/pallas_call | solution.py:70
  116.7 5.5 %shard_map.274 = f32[2,128]{1,0:T(2,128)} custom-call(f32[2,128]{1,0:T(2,128)} %bitcast.465), custom_call_target="tpu_custom_call" | custom-call | tf_op jit(solution)/shard_map/pallas_call | solution.py:70
  125.1 13.8 %shard_map.275 = f32[64,768]{1,0:T(8,128)} custom-call(bf16[4,64,768]{2,1,0:T(8,128)(2,1)} %bitcast.377), custom_call_target="tpu_custom_call" | custom-call | tf_op jit(solution)/shard_map/pallas_call | solution.py:70
  140.8 12.9 %shard_map.276 = bf16[4,64,768]{2,1,0:T(8,128)(2,1)} custom-call(bf16[64,768]{1,0:T(8,128)(2,1)} %multiply_convert_fusion.4.refs_0_), custom_call_target="tpu_custom_call" | custom-call | tf_op jit(solution)/shard_map/pallas_call | solution.py:70
  164.9 3.5 collective-permute-start.2
  174.6 13.0 %shard_map.277 = (f32[8,1,128]{2,1,0:T(1,128)}, bf16[8,384,128]{2,1,0:T(8,128)(2,1)}) custom-call(f32[1,128]{1,0:T(1,128)} %pad_bitcast_fusion.1.refs_0_, bf16[384,128]{1,0:T(8,128)(2,1)} %bitcast.435), custom_call_target="tpu_custom_call" | custom-call | tf_op jit(solution)/shard_map/pallas_call | solution.py:70
  198.0 5.4 %shard_map.278 = f32[2,128]{1,0:T(2,128)} custom-call(f32[2,128]{1,0:T(2,128)} %bitcast.466), custom_call_target="tpu_custom_call" | custom-call | tf_op jit(solution)/shard_map/pallas_call | solution.py:70
  204.1 2.8 multiply_reduce_fusion.12
  206.9 5.8 %shard_map.281 = f32[2,128]{1,0:T(2,128)} custom-call(f32[2,128]{1,0:T(2,128)} %bitcast.473), custom_call_target="tpu_custom_call" | custom-call | tf_op jit(solution)/shard_map/pallas_call | solution.py:70
  213.4 3.0 multiply_reduce_fusion.10
  221.5 14.8 %shard_map.282 = bf16[8,384,128]{2,1,0:T(8,128)(2,1)} custom-call(bf16[384,128]{1,0:T(8,128)(2,1)} %bitcast.436), custom_call_target="tpu_custom_call" | custom-call | tf_op jit(solution)/shard_map/pallas_call | solution.py:70
  243.4 3.4 fusion.68
  253.8 2.4 multiply_reduce_fusion.18
  275.6 2.4 fusion.454
  278.0 2.4 convolution_convert_fusion.2
  286.3 12.8 %shard_map.279 = f32[64,768]{1,0:T(8,128)} custom-call(bf16[4,64,768]{2,1,0:T(8,128)(2,1)} %bitcast.376), custom_call_target="tpu_custom_call" | custom-call | tf_op jit(solution)/shard_map/pallas_call | solution.py:70
  303.8 13.5 %shard_map.283 = f32[64,768]{1,0:T(8,128)} custom-call(bf16[4,64,768]{2,1,0:T(8,128)(2,1)} %bitcast.431), custom_call_target="tpu_custom_call" | custom-call | tf_op jit(solution)/shard_map/pallas_call | solution.py:70
  320.8 13.6 %shard_map.284 = bf16[4,64,768]{2,1,0:T(8,128)(2,1)} custom-call(bf16[64,768]{1,0:T(8,128)(2,1)} %fusion.449.refs_0_), custom_call_target="tpu_custom_call" | custom-call | tf_op jit(solution)/shard_map/pallas_call | solution.py:70
  334.5 2.9 multiply_reduce_fusion.13
  337.4 4.7 shard_map.285
  342.7 2.8 multiply_reduce_fusion.11
  348.8 15.2 %shard_map.286 = bf16[8,384,128]{2,1,0:T(8,128)(2,1)} custom-call(bf16[384,128]{1,0:T(8,128)(2,1)} %bitcast.437), custom_call_target="tpu_custom_call" | custom-call | tf_op jit(solution)/shard_map/pallas_call | solution.py:70
  364.1 2.4 fusion.70
  372.7 2.4 multiply_reduce_fusion.14
  418.7 12.7 %shard_map.287 = f32[64,768]{1,0:T(8,128)} custom-call(bf16[4,64,768]{2,1,0:T(8,128)(2,1)} %bitcast.430), custom_call_target="tpu_custom_call" | custom-call | tf_op jit(solution)/shard_map/pallas_call | solution.py:70
  438.8 2.5 pad_maximum_fusion
  441.3 62.7 %shard_map.288 = (f32[96,1536]{1,0:T(8,128)}, f32[96,1536]{1,0:T(8,128)}, f32[72,128]{1,0:T(8,128)}) custom-call(bf16[8,96,1536]{2,1,0:T(8,128)(2,1)} %bitcast.343, bf16[8,96,1536]{2,1,0:T(8,128)(2,1)} %bitcast.342, f32[72,128]{1,0:T(8,128)} %pad_bitcast_fusion.refs_2_), custom_call_target="tpu_custom_call" | custom-call | tf_op jit(solution)/shard_map/pallas_call | solution.py:70
  506.7 16.3 %shard_map.289 = (f32[4,72,128]{2,1,0:T(8,128)}, f32[2,96,256]{2,1,0:T(8,128)}) custom-call(f32[72,128]{1,0:T(8,128)} %get-tuple-element.36.refs_0_, bf16[2,96,256]{2,1,0:T(8,128)(2,1)} %fusion.151.refs_1_), custom_call_target="tpu_custom_call" | custom-call | tf_op jit(solution)/shard_map/pallas_call | solution.py:70
  (766 shorter events, 188.8 us)
Async XLA Ops:
  7.2 153.9 %all-gather.2.cloned.1.call-start = ((), (), s32[]{:S(2)}) async-start(), calls=%async_computation | async-start | bytes 2654208 | tf_op jit(solution)/shard_map/all_gather | solution.py:236
  11.1 32.5 %copy-start.189 = (f32[2,768]{1,0:T(2,128)S(1)}, f32[2,768]{1,0:T(2,128)}, u32[]{:S(2)}) copy-start(f32[2,768]{1,0:T(2,128)} %param.19) | copy-start | bytes 18436
  11.1 32.6 %copy-start.39 = (bf16[64,768]{1,0:T(8,128)(2,1)S(1)}, bf16[64,768]{1,0:T(8,128)(2,1)}, u32[]{:S(2)}) copy-start(bf16[64,768]{1,0:T(8,128)(2,1)} %param.17) | copy-start | bytes 294916
  60.8 55.1 %copy-start.27 = (f32[256,1152]{1,0:T(8,128)}, f32[256,1152]{1,0:T(8,128)S(1)}, u32[]{:S(2)}) copy-start(f32[256,1152]{1,0:T(8,128)S(1)} %get-tuple-element.295) | copy-start | bytes 3538948
  60.9 32.4 %collective-permute-start = (bf16[3,640]{1,0:T(4,128)(2,1)S(1)}, bf16[3,640]{1,0:T(4,128)(2,1)S(1)}, u32[]{:S(2)}, u32[]{:S(2)}) collective-permute-start(bf16[3,640]{1,0:T(4,128)(2,1)S(1)} %slice.732), channel_id=1, source_target_pairs={{0,4},{4,8},{8,12},{12,16},{16,20},{20,24},{24,28},{1,5},{5,9},{9,... | collective-permute-start | bytes 11528 | tf_op jit(solution)/shard_map/ppermute | solution.py:106
  63.6 23.8 %collective-permute-start.1 = (bf16[3]{0:T(256)(128)(2,1)S(1)}, bf16[3]{0:T(256)(128)(2,1)S(1)}, u32[]{:S(2)}, u32[]{:S(2)}) collective-permute-start(bf16[3]{0:T(256)(128)(2,1)S(1)} %add_convert_fusion.1), channel_id=1, source_target_pairs={{0,4},{4,8},{8,12},{12,16},{16,20},{20,24},{24,28},{1,5},{5,9},{9,... | collective-permute-start | bytes 26 | tf_op jit(solution)/shard_map/ppermute | solution.py:106
  67.3 47.1 %copy-start.91 = (pred[256,256]{1,0:T(8,128)(4,1)}, pred[256,256]{1,0:T(8,128)(4,1)S(1)}, u32[]{:S(2)}) copy-start(pred[256,256]{1,0:T(8,128)(4,1)S(1)} %fusion.139) | copy-start | bytes 196612
  70.4 52.4 %copy-start.116 = (f32[384]{0:T(512)}, f32[384]{0:T(512)S(1)}, u32[]{:S(2)}) copy-start(f32[384]{0:T(512)S(1)} %get-tuple-element.155) | copy-start | bytes 4612
  111.2 49.2 %copy-start.201 = (f32[6]{0:T(128)}, f32[6]{0:T(128)S(1)}, u32[]{:S(2)}) copy-start(f32[6]{0:T(128)S(1)} %get-tuple-element.263) | copy-start | bytes 76
  112.1 41.5 %copy-start.171 = (f32[6]{0:T(128)}, f32[6]{0:T(128)S(1)}, u32[]{:S(2)}) copy-start(f32[6]{0:T(128)S(1)} %get-tuple-element.261) | copy-start | bytes 76
  112.1 42.3 %copy-start.169 = (f32[6]{0:T(128)}, f32[6]{0:T(128)S(1)}, u32[]{:S(2)}) copy-start(f32[6]{0:T(128)S(1)} %get-tuple-element.260) | copy-start | bytes 76
  112.2 43.0 %copy-start.167 = (f32[6]{0:T(128)}, f32[6]{0:T(128)S(1)}, u32[]{:S(2)}) copy-start(f32[6]{0:T(128)S(1)} %get-tuple-element.259) | copy-start | bytes 76
  112.2 43.8 %copy-start.165 = (f32[6]{0:T(128)}, f32[6]{0:T(128)S(1)}, u32[]{:S(2)}) copy-start(f32[6]{0:T(128)S(1)} %get-tuple-element.258) | copy-start | bytes 76
  112.2 44.5 %copy-start.163 = (f32[6]{0:T(128)}, f32[6]{0:T(128)S(1)}, u32[]{:S(2)}) copy-start(f32[6]{0:T(128)S(1)} %get-tuple-element.257) | copy-start | bytes 76
  112.2 45.2 %copy-start.161 = (f32[6]{0:T(128)}, f32[6]{0:T(128)S(1)}, u32[]{:S(2)}) copy-start(f32[6]{0:T(128)S(1)} %get-tuple-element.256) | copy-start | bytes 76
  112.2 46.7 %copy-start.198 = (f32[6]{0:T(128)}, f32[6]{0:T(128)S(1)}, u32[]{:S(2)}) copy-start(f32[6]{0:T(128)S(1)} %get-tuple-element.255) | copy-start | bytes 76
  116.7 37.0 %copy-start.18 = (f32[256,384]{1,0:T(8,128)}, f32[256,384]{1,0:T(8,128)S(1)}, u32[]{:S(2)}) copy-start(f32[256,384]{1,0:T(8,128)S(1)} %get-tuple-element.181) | copy-start | bytes 1179652
  140.0 179.0 %copy-start.23 = (f32[64,768]{1,0:T(8,128)}, f32[64,768]{1,0:T(8,128)S(1)}, u32[]{:S(2)}) copy-start(f32[64,768]{1,0:T(8,128)S(1)} %get-tuple-element.179) | copy-start | bytes 589828
  164.2 89.4 %copy-start.89 = (f32[256,6]{0,1:T(8,128)}, f32[256,6]{0,1:T(8,128)S(1)}, u32[]{:S(2)}) copy-start(f32[256,6]{0,1:T(8,128)S(1)} %fusion.137) | copy-start | bytes 18436
  164.9 7.0 %collective-permute-start.2 = (bf16[3,640]{1,0:T(4,128)(2,1)S(1)}, bf16[3,640]{1,0:T(4,128)(2,1)S(1)}, u32[]{:S(2)}, u32[]{:S(2)}) collective-permute-start(bf16[3,640]{1,0:T(4,128)(2,1)S(1)} %slice.752), channel_id=1, source_target_pairs={{0,4},{4,8},{8,12},{12,16},{16,20},{20,24},{24,28},{1,5},{5,9},{9,... | collective-permute-start | bytes 11528 | tf_op jit(solution)/shard_map/ppermute | solution.py:106
  189.2 48.4 %copy-start.177 = (f32[6]{0:T(128)}, f32[6]{0:T(128)S(1)}, u32[]{:S(2)}) copy-start(f32[6]{0:T(128)S(1)} %get-tuple-element.268) | copy-start | bytes 76
  189.2 48.6 %copy-start.175 = (f32[6]{0:T(128)}, f32[6]{0:T(128)S(1)}, u32[]{:S(2)}) copy-start(f32[6]{0:T(128)S(1)} %get-tuple-element.267) | copy-start | bytes 76
  198.0 38.4 %copy-start.21 = (f32[256,384]{1,0:T(8,128)}, f32[256,384]{1,0:T(8,128)S(1)}, u32[]{:S(2)}) copy-start(f32[256,384]{1,0:T(8,128)S(1)} %get-tuple-element.175) | copy-start | bytes 1179652
  262.4 36.7 %collective-permute-start.3 = (f32[3,640]{1,0:T(4,128)}, f32[3,640]{1,0:T(4,128)}, u32[]{:S(2)}, u32[]{:S(2)}) collective-permute-start(f32[3,640]{1,0:T(4,128)} %pad_add_fusion.3), channel_id=1, source_target_pairs={{4,0},{8,4},{12,8},{16,12},{20,16},{24,20},{28,24},{5,1},{9,5},{13... | collective-permute-start | bytes 23048 | tf_op jit(solution)/shard_map/ppermute | solution.py:106
  303.8 30.6 %copy-start.19 = (f32[256,384]{1,0:T(8,128)S(1)}, f32[256,384]{1,0:T(8,128)}, u32[]{:S(2)}) copy-start(f32[256,384]{1,0:T(8,128)} %copy-done.18) | copy-start | bytes 1179652
  303.8 30.6 %copy-start.117 = (f32[384]{0:T(512)S(1)}, f32[384]{0:T(512)}, u32[]{:S(2)}) copy-start(f32[384]{0:T(512)} %copy-done.116) | copy-start | bytes 4612
  303.8 30.6 %copy-start.132 = (f32[256]{0:T(256)S(1)}, f32[256]{0:T(256)}, u32[]{:S(2)}) copy-start(f32[256]{0:T(256)} %copy-done.131) | copy-start | bytes 3076
  385.9 26.4 %collective-permute-start.4 = (f32[3,640]{1,0:T(4,128)}, f32[3,640]{1,0:T(4,128)}, u32[]{:S(2)}, u32[]{:S(2)}) collective-permute-start(f32[3,640]{1,0:T(4,128)} %pad_add_fusion.2), channel_id=1, source_target_pairs={{4,0},{8,4},{12,8},{16,12},{20,16},{24,20},{28,24},{5,1},{9,5},{13... | collective-permute-start | bytes 23048 | tf_op jit(solution)/shard_map/ppermute | solution.py:106
  506.0 26.1 %copy-start.218 = (f32[64]{0:T(128)S(1)}, f32[64]{0:T(128)}, u32[]{:S(2)}) copy-start(f32[64]{0:T(128)} %get-tuple-element.143) | copy-start | bytes 772
  506.0 26.0 %copy-start.24 = (f32[64,768]{1,0:T(8,128)S(1)}, f32[64,768]{1,0:T(8,128)}, u32[]{:S(2)}) copy-start(f32[64,768]{1,0:T(8,128)} %copy-done.23) | copy-start | bytes 589828
  506.0 26.0 %copy-start.32 = (f32[64,768]{1,0:T(8,128)S(1)}, f32[64,768]{1,0:T(8,128)}, u32[]{:S(2)}) copy-start(f32[64,768]{1,0:T(8,128)} %shard_map.283) | copy-start | bytes 589828
  506.0 26.0 %copy-start.40 = (bf16[64,768]{1,0:T(8,128)(2,1)S(1)}, bf16[64,768]{1,0:T(8,128)(2,1)}, u32[]{:S(2)}) copy-start(bf16[64,768]{1,0:T(8,128)(2,1)} %param.17) | copy-start | bytes 294916
  (203 other events, 1273.2 us)
Sparse Core Ops, SparseCore 0:
  66.7 28.5 all-gather.1

commit v2 on v1

--- a/solution.py
+++ b/solution.py
@@ -11,12 +11,35 @@
 MESH = pl.DeviceIdType.MESH
 
 
-def exchange(parts, axis, collective_id):
-    count = lax.axis_size(axis)
+def add_up(slots, result, count):
+    rows = result.shape[0]
+    tile = 32
+
+    def some(rows_of):
+        total = slots[(0, *rows_of)].astype(jnp.float32)
+        for source in range(1, count):
+            total = total + slots[(source, *rows_of)].astype(jnp.float32)
+        result[rows_of] = total
+
+    if result.ndim == 2 and rows % tile == 0 and rows > tile:
+
+        @pl.loop(0, rows // tile)
+        def _(index):
+            some((pl.ds(pl.multiple_of(index * tile, tile), tile), slice(None)))
+
+    else:
+        some((slice(None),) * result.ndim)
+
+
+def exchange(parts, collective_id):
+    axes = sorted({axis for _, axis, _, _ in parts})
+    counts = {axis: lax.axis_size(axis) for axis in axes}
+    most = max(counts.values())
     many = len(parts)
-    block_shapes = [a.shape[1:] if scatter else a.shape for a, scatter, _ in parts]
+    block_shapes = [a.shape[1:] if scatter else a.shape for a, _, scatter, _ in parts]
     outs, slots = [], []
-    for (a, _, reduce), shape in zip(parts, block_shapes):
+    for (a, axis, _, reduce), shape in zip(parts, block_shapes):
+        count = counts[axis]
         if reduce:
             outs.append(jax.ShapeDtypeStruct(shape, jnp.float32))
             slots.append(pltpu.VMEM((count,) + shape, a.dtype))
@@ -28,24 +51,29 @@
         scratch = list(refs[2 * many : len(refs) - 3])
         send_sem, recv_sem, own_sem = refs[len(refs) - 3 :]
         landing = [
-            scratch.pop(0) if reduce else results[i] for i, (_, _, reduce) in enumerate(parts)
+            scratch.pop(0) if reduce else results[i] for i, (_, _, _, reduce) in enumerate(parts)
         ]
-        me = lax.axis_index(axis)
+        places = {axis: lax.axis_index(axis) for axis in axes}
         barrier = pltpu.get_barrier_semaphore()
-        for step in range(1, count):
-            peer = lax.rem(me + step, count)
-            pl.semaphore_signal(barrier, inc=1, device_id={axis: peer}, device_id_type=MESH)
+        for axis in axes:
+            for step in range(1, counts[axis]):
+                peer = lax.rem(places[axis] + step, counts[axis])
+                pl.semaphore_signal(barrier, inc=1, device_id={axis: peer}, device_id_type=MESH)
         own = []
-        for i, (_, scatter, _) in enumerate(parts):
+        for i, (_, axis, scatter, _) in enumerate(parts):
+            me = places[axis]
             block = ins[i].at[me] if scatter else ins[i]
             copy = pltpu.make_async_copy(block, landing[i].at[me], own_sem.at[i])
             copy.start()
             own.append(copy)
-        pl.semaphore_wait(barrier, count - 1)
+        pl.semaphore_wait(barrier, sum(counts[axis] - 1 for axis in axes))
         sent = []
-        for step in range(1, count):
-            peer = lax.rem(me + step, count)
-            for i, (_, scatter, _) in enumerate(parts):
+        for step in range(1, most):
+            for i, (_, axis, scatter, _) in enumerate(parts):
+                if step >= counts[axis]:
+                    continue
+                me = places[axis]
+                peer = lax.rem(me + step, counts[axis])
                 copy = pltpu.make_async_remote_copy(
                     src_ref=ins[i].at[peer] if scatter else ins[i],
                     dst_ref=landing[i].at[me],
@@ -60,12 +88,9 @@
             copy.wait()
         for copy in sent:
             copy.wait()
-        for i, (_, _, reduce) in enumerate(parts):
+        for i, (_, axis, _, reduce) in enumerate(parts):
             if reduce:
-                total = landing[i][0].astype(jnp.float32)
-                for source in range(1, count):
-                    total = total + landing[i][source].astype(jnp.float32)
-                results[i][...] = total
+                add_up(landing[i], results[i], counts[axis])
 
     return pl.pallas_call(
         kernel,
@@ -74,30 +99,29 @@
         out_specs=tuple([pl.BlockSpec(memory_space=pltpu.VMEM)] * many),
         scratch_shapes=slots
         + [
-            pltpu.SemaphoreType.DMA((many, count - 1)),
-            pltpu.SemaphoreType.DMA((many, count - 1)),
+            pltpu.SemaphoreType.DMA((many, most - 1)),
+            pltpu.SemaphoreType.DMA((many, most - 1)),
             pltpu.SemaphoreType.DMA((many,)),
         ],
         compiler_params=pltpu.CompilerParams(collective_id=collective_id, has_side_effects=True),
-    )(*[a for a, _, _ in parts])
-
-
-def rows_from_all(rows, collective_id):
-    (out,) = exchange([(rows, False, False)], "tensor", collective_id)
-    return out.reshape(-1, rows.shape[1])
-
-
-def rows_summed(partial_rows, collective_id):
+    )(*[a for a, _, _, _ in parts])
+
+
+def rows_from_all(rows, collective_id, extra=()):
+    out, *others = exchange([(rows, "tensor", False, False), *extra], collective_id)
+    return (out.reshape(-1, rows.shape[1]), others)
+
+
+def rows_summed(partial_rows, collective_id, extra=()):
     count = lax.axis_size("tensor")
     blocks = partial_rows.astype(jnp.bfloat16).reshape(count, -1, partial_rows.shape[1])
-    return exchange([(blocks, True, True)], "tensor", collective_id)[0]
-
-
-def token_sums(values, collective_id):
-    length = values.shape[0]
-    return exchange([(values.reshape(-1, 128), False, True)], "tensor", collective_id)[0].reshape(
-        length
-    )
+    out, *others = exchange([(blocks, "tensor", True, True), *extra], collective_id)
+    return (out, others)
+
+
+def token_sums(values, collective_id, extra=()):
+    out, *others = exchange([(values.reshape(-1, 128), "tensor", False, True), *extra], collective_id)
+    return (out.reshape(values.shape[0]), others)
 
 
 def passed_along(block, axis, distance):
@@ -212,7 +236,6 @@
     at_bc = 2 * local_inner
     at_dt = at_bc + state_pair
     at_out = at_dt + dt_room
-    width = at_out + local_inner
     ids = iter(range(1, 64))
 
     packed = [
@@ -221,19 +244,17 @@
                 w_zx[l].reshape(-1, at_bc),
                 w_bc[l],
                 jnp.pad(w_dt[l], ((0, 0), (0, dt_room - local_heads))),
-                w_out[l].T,
             ],
             axis=1,
         )
         for l in range(layers)
     ]
-    weights_all = []
-    for l in range(layers):
-        if l == 0:
-            (full,) = exchange([(packed[l], False, False)], "dp", next(ids))
-            weights_all.append(full.reshape(model_width, width))
-        else:
-            weights_all.append(lax.all_gather(packed[l], "dp", axis=0, tiled=True))
+    later_weights = [
+        lax.all_gather(
+            jnp.concatenate([packed[l], w_out[l].T], axis=1), "dp", axis=0, tiled=True
+        )
+        for l in range(1, layers)
+    ]
 
     seg_tail = (segment_ids[shard_rows - margin :] + 1).astype(jnp.bfloat16)
     tail_segs = passed_along(seg_tail, "dp", 1)
@@ -244,11 +265,20 @@
     hidden = x_in.astype(jnp.float32)
     records = []
     for layer_num in range(layers):
-        weights = weights_all[layer_num]
         rms_scale = lax.rsqrt(jnp.mean(hidden * hidden, axis=1, keepdims=True) + EPSILON)
         normed = (hidden * rms_scale * norm_gain[layer_num]).astype(jnp.bfloat16)
-        gathered = rows_from_all(normed, next(ids))
-        projected = jnp.dot(gathered, weights[:, :at_out], preferred_element_type=jnp.float32)
+        if layer_num == 0:
+            gathered, (w_in,) = rows_from_all(
+                normed, next(ids), [(packed[0], "dp", False, False)]
+            )
+            w_in = w_in.reshape(model_width, at_out)
+            ride = [(w_out[0].T, "dp", False, False)]
+        else:
+            gathered, _ = rows_from_all(normed, next(ids))
+            full = later_weights[layer_num - 1]
+            w_in, w_back = full[:, :at_out], full[:, at_out:]
+            ride = []
+        projected = jnp.dot(gathered, w_in, preferred_element_type=jnp.float32)
         proj_z = projected[:, :local_inner]
         proj_dt = projected[:, at_dt : at_dt + local_heads]
         conv_in = projected[:, local_inner:at_dt].astype(jnp.bfloat16)
@@ -293,18 +323,25 @@
         local_y, local_state, cumulative = core_vals
         end_decay = jnp.exp(cumulative[shard_rows - 1])
         coefficient = joined * whole_seg * end_decay
-        coefficients, states = exchange(
-            [
-                (jnp.pad(coefficient, (0, dt_room - local_heads)).reshape(-1, 128), False, False),
-                (
-                    local_state.astype(jnp.bfloat16).reshape(local_inner, state_width),
-                    False,
-                    False,
-                ),
-            ],
-            "dp",
-            next(ids),
-        )
+        pieces = [
+            (
+                jnp.pad(coefficient, (0, dt_room - local_heads)).reshape(-1, 128),
+                "dp",
+                False,
+                False,
+            ),
+            (
+                local_state.astype(jnp.bfloat16).reshape(local_inner, state_width),
+                "dp",
+                False,
+                False,
+            ),
+        ]
+        if layer_num == 0:
+            pieces.append((cotangent, "tensor", False, False))
+        coefficients, states, *others = exchange(pieces, next(ids))
+        if layer_num == 0:
+            last_branch_grad = others[0].reshape(-1, model_width)
         coefficients = coefficients.reshape(data_count, dt_room)[:, :local_heads]
         states = states.reshape(data_count, local_heads, head_width, state_width)
         start_state = joined * entering(coefficients, states, False)
@@ -314,20 +351,24 @@
         ssd_y = (local_y + init_y).reshape(shard_rows, local_inner)
         gate_vals = jax.nn.silu(proj_z)
         gated_y = ssd_y * gate_vals
-        squares = token_sums(jnp.sum(gated_y * gated_y, axis=1), next(ids))
+        squares, others = token_sums(jnp.sum(gated_y * gated_y, axis=1), next(ids), ride)
+        if layer_num == 0:
+            w_back = others[0].reshape(model_width, local_inner)
         inverse = lax.rsqrt(squares / full_inner + EPSILON)
         mixed_out = (gated_y * inverse[:, None] * gate_gain[layer_num]).astype(jnp.bfloat16)
-        branch = rows_summed(
+        branch, _ = rows_summed(
             jnp.einsum(
                 "tk,dk->td",
                 mixed_out,
-                weights[:, at_out:],
+                w_back,
                 preferred_element_type=jnp.float32,
             ),
             next(ids),
         )
         records.append(
             (
+                w_in,
+                w_back,
                 hidden,
                 gathered,
                 proj_z,
@@ -347,10 +388,18 @@
         hidden = hidden + branch
     y_out = hidden.astype(jnp.bfloat16)
     grad_hidden = cotangent.astype(jnp.float32)
-    weight_grads = [None] * layers
+
+    def by_owner(grad):
+        blocks = grad.astype(jnp.bfloat16).reshape(data_count, -1, grad.shape[1])
+        return (blocks, "dp", True, True)
+
     small_grads = [None] * layers
+    waiting = []
+    summed = {}
     for layer_num in reversed(range(layers)):
         (
+            w_in,
+            w_back,
             hidden_in,
             gathered,
             proj_z,
@@ -366,14 +415,25 @@
             core_back,
             init_back,
         ) = records[layer_num]
-        weights = weights_all[layer_num]
-        branch_grad = rows_from_all(grad_hidden.astype(jnp.bfloat16), next(ids))
+        riders = waiting[:2]
+        if layer_num == layers - 1:
+            branch_grad = last_branch_grad
+        else:
+            branch_grad, others = rows_from_all(
+                grad_hidden.astype(jnp.bfloat16), next(ids), [r[1] for r in riders]
+            )
+            summed.update(zip([r[0] for r in riders], others))
+        waiting = waiting[2:]
         d_out = jnp.einsum("td,tk->dk", branch_grad, mixed_out, preferred_element_type=jnp.float32)
         d_mixed = jnp.einsum(
-            "td,dk->tk", branch_grad, weights[:, at_out:], preferred_element_type=jnp.float32
+            "td,dk->tk", branch_grad, w_back, preferred_element_type=jnp.float32
         )
         weighted = d_mixed * gate_gain[layer_num]
-        inner_dot = token_sums(jnp.sum(weighted * gated_y, axis=1), next(ids))
+        riders, waiting = waiting[:1], waiting[1:]
+        inner_dot, others = token_sums(
+            jnp.sum(weighted * gated_y, axis=1), next(ids), [r[1] for r in riders]
+        )
+        summed.update(zip([r[0] for r in riders], others))
         d_gated = (
             inverse[:, None] * weighted
             - gated_y * (inverse * inverse * inverse * inner_dot / full_inner)[:, None]
@@ -390,11 +450,11 @@
             [
                 (
                     (joined * d_start).astype(jnp.bfloat16).reshape(local_inner, state_width),
+                    "dp",
                     False,
                     False,
                 )
             ],
-            "dp",
             next(ids),
         )
         d_end = entering(
@@ -429,26 +489,27 @@
             ],
             axis=1,
         )
-        d_normed = rows_summed(
+        waiting.append(((layer_num, 3), by_owner(d_out)))
+        riders, waiting = waiting[:2], waiting[2:]
+        d_normed, others = rows_summed(
             jnp.einsum(
-                "tk,dk->td", d_all, weights[:, :at_out], preferred_element_type=jnp.float32
+                "tk,dk->td", d_all, w_in, preferred_element_type=jnp.float32
             )
             + jnp.einsum(
-                "tk,dk->td", bc_rest, weights[:, at_bc:at_dt], preferred_element_type=jnp.float32
+                "tk,dk->td", bc_rest, w_in[:, at_bc:at_dt], preferred_element_type=jnp.float32
             ),
             next(ids),
-        )
+            [r[1] for r in riders],
+        )
+        summed.update(zip([r[0] for r in riders], others))
         d_in = jnp.einsum("td,tk->dk", gathered, d_all, preferred_element_type=jnp.float32)
         d_rest = jnp.einsum("td,tk->dk", gathered, bc_rest, preferred_element_type=jnp.float32)
-        weight_grads[layer_num] = jnp.concatenate(
-            [
-                d_in[:, :at_bc].astype(jnp.bfloat16),
-                (d_in[:, at_bc:at_dt] + d_rest).astype(jnp.bfloat16),
-                d_in[:, at_dt:].astype(jnp.bfloat16),
-                d_out.astype(jnp.bfloat16),
-            ],
-            axis=1,
-        ).reshape(data_count, model_width // data_count, width)
+        d_maps = jnp.concatenate([d_in[:, at_bc:at_dt] + d_rest, d_in[:, at_dt:]], axis=1)
+        waiting += [
+            ((layer_num, 0), by_owner(d_in[:, :local_inner])),
+            ((layer_num, 1), by_owner(d_in[:, local_inner:at_bc])),
+            ((layer_num, 2), by_owner(d_maps)),
+        ]
         rms_scale = lax.rsqrt(jnp.mean(hidden_in * hidden_in, axis=1, keepdims=True) + EPSILON)
         gain_grad_in = d_normed * norm_gain[layer_num]
         d_norm_gain = jnp.sum(d_normed * hidden_in * rms_scale, axis=0)
@@ -476,13 +537,14 @@
     small = [jnp.stack([small_grads[l][m] for l in range(layers)]) for m in range(9)]
     flat = jnp.concatenate([s.reshape(-1) for s in small])
     flat = jnp.pad(flat, (0, -flat.shape[0] % 1024)).reshape(-1, 128)
-    reduced = exchange(
-        [(g, True, True) for g in weight_grads] + [(flat, False, True)], "dp", next(ids)
+    flat, *others = exchange(
+        [(flat, "dp", False, True)] + [r[1] for r in waiting], next(ids)
     )
-    grads, flat = jnp.stack(reduced[:layers]), reduced[layers]
-    d_bc = grads[:, :, at_bc:at_dt].astype(jnp.bfloat16)
+    summed.update(zip([r[0] for r in waiting], others))
+    grads = [jnp.stack([summed[(l, m)] for l in range(layers)]) for m in range(4)]
+    d_bc = grads[2][:, :, :state_pair].astype(jnp.bfloat16)
     flats, bc_total = exchange(
-        [(flat, False, False), (d_bc, False, True)], "tensor", next(ids)
+        [(flat, "tensor", False, False), (d_bc, "tensor", False, True)], next(ids)
     )
     flats = flats.reshape(tensor_count, -1)
     totals, start = [], 0
@@ -498,8 +560,8 @@
         y_out,
         grad_hidden,
         totals[8],
-        grads[:, :, :at_bc].reshape(layers, -1, 2, local_inner),
-        grads[:, :, at_dt : at_dt + local_heads],
+        jnp.stack([grads[0], grads[1]], axis=2),
+        grads[2][:, :, state_pair : state_pair + local_heads],
         bc_total,
         totals[0],
         totals[1],
@@ -509,7 +571,7 @@
         totals[4],
         totals[5],
         totals[2],
-        jnp.swapaxes(grads[:, :, at_out:], 1, 2),
+        jnp.swapaxes(grads[3], 1, 2),
     )
 
 

time: 552 us -> 485 us (0.88); the launches traced: 541 us -> 481 us
  Pallas kernels: 296 us -> 257 us
  local copies, waits for them, and re-layouts: 93.5 us -> 70.2 us
  starting transfers between devices: 12.4 us -> 24.1 us
  other arithmetic: 66 us -> 57.1 us
    pallas_call x19 -> x17, Pallas kernels: 296 us -> 257 us  [exchange(): pl.pallas_call(kernel, out_shape=tuple(outs), in_specs=[pl.BlockSpec(memo...]
    ppermute x5, starting transfers between devices: 12.4 us -> 24.1 us  [passed_along(): return lax.ppermute(block, axis, route)]
    mul x42, local copies, waits for them, and re-layouts: 16.9 us -> 11.3 us  [entering(): coefficients[source][:, None, None] * state]
    unnamed x468 -> x469, local copies, waits for them, and re-layouts: 14.2 us -> 13 us
  transfers between devices with their start and end apart: 6 -> 6, of which waited for: 0 -> 0; matrix products, arithmetic and copies ran while one was open for 15% -> 11% of each run, Pallas kernels for 13% -> 15%
where the time goes in v2:
time: 485 us; the launch traced here: 481 us
  Pallas kernels  257 us (53%)
  local copies, waits for them, and re-layouts  70.2 us (14%)
  other arithmetic  57.1 us (12%)
  matrix products  51.4 us (11%)
  starting transfers between devices  24.1 us (5%)
  between operations  20.4 us (4%)
    pallas_call x17, Pallas kernels, exchange(): pl.pallas_call(kernel, out_shape=tuple(outs), in_specs=[pl.BlockSpec(memo...  257 us
    ppermute x5, starting transfers between devices, passed_along(): return lax.ppermute(block, axis, route)  24.1 us
    unnamed x469, local copies, waits for them, and re-layouts  13 us
    dot_general x6, matrix products, mixer_core(): jnp.einsum('hij,jhp->ihp', decays * scores[None], scaled, precision=CORE)  11.6 us
    mul x42, local copies, waits for them, and re-layouts, entering(): coefficients[source][:, None, None] * state  11.3 us
  transfers between devices with their start and end apart: 6, of which 0 were waited for; matrix products, arithmetic and copies ran while one was open for 11% of the time, Pallas kernels for 15%

profile of v2, /device:TPU:9, one launch (start us, length us, event | category | flops | bytes accessed | tf_op | source)
XLA Modules:
  0.0 480.6 jit_solution(6054521582052888742)
XLA Ops:
  14.3 26.1 %shard_map.271 = (bf16[4,64,768]{2,1,0:T(8,128)(2,1)}, bf16[8,96,1152]{2,1,0:T(8,128)(2,1)}) custom-call(bf16[64,768]{1,0:T(8,128)(2,1)} %fusion.126.refs_0_, bf16[96,1152]{1,0:T(8,128)(2,1)} %fusion.125.refs_1_), custom_call_target="tpu_custom_call" | custom-call | tf_op jit(solution)/shard_map/pallas_call | solution.py:95
  40.5 2.3 fusion.452
  45.1 3.5 collective-permute-start.1
  66.6 20.3 %shard_map.272 = (f32[8,1,128]{2,1,0:T(1,128)}, bf16[8,384,128]{2,1,0:T(8,128)(2,1)}, bf16[4,64,768]{2,1,0:T(8,128)(2,1)}) custom-call(f32[1,128]{1,0:T(1,128)} %pad_bitcast_fusion.2.refs_0_, bf16[384,128]{1,0:T(8,128)(2,1)} %bitcast.455, bf16[64,768]{1,0:T(8,128)(2,1)} %refs_2_.1), custom_call_target="tpu_custom_call" | custom-call | tf_op jit(solution)/shard_map/pallas_call | solution.py:95
  93.2 11.9 %shard_map.273 = (f32[2,128]{1,0:T(2,128)}, bf16[8,96,384]{2,1,0:T(8,128)(2,1)}) custom-call(f32[2,128]{1,0:T(2,128)} %bitcast.496, bf16[96,384]{1,0:T(8,128)(2,1)} %get-tuple-element.275.refs_1_), custom_call_target="tpu_custom_call" | custom-call | tf_op jit(solution)/shard_map/pallas_call | solution.py:95
  108.0 13.3 %shard_map.274 = f32[64,768]{1,0:T(8,128)} custom-call(bf16[4,64,768]{2,1,0:T(8,128)(2,1)} %bitcast.393), custom_call_target="tpu_custom_call" | custom-call | tf_op jit(solution)/shard_map/pallas_call | solution.py:95
  123.1 13.6 %shard_map.275 = bf16[4,64,768]{2,1,0:T(8,128)(2,1)} custom-call(bf16[64,768]{1,0:T(8,128)(2,1)} %multiply_convert_fusion.4.refs_0_), custom_call_target="tpu_custom_call" | custom-call | tf_op jit(solution)/shard_map/pallas_call | solution.py:95
  144.1 2.3 fusion.453
  147.6 3.4 collective-permute-start.2
  158.1 13.4 %shard_map.276 = (f32[8,1,128]{2,1,0:T(1,128)}, bf16[8,384,128]{2,1,0:T(8,128)(2,1)}) custom-call(f32[1,128]{1,0:T(1,128)} %pad_bitcast_fusion.1.refs_0_, bf16[384,128]{1,0:T(8,128)(2,1)} %bitcast.456), custom_call_target="tpu_custom_call" | custom-call | tf_op jit(solution)/shard_map/pallas_call | solution.py:95
  179.7 5.6 %shard_map.277 = f32[2,128]{1,0:T(2,128)} custom-call(f32[2,128]{1,0:T(2,128)} %bitcast.497), custom_call_target="tpu_custom_call" | custom-call | tf_op jit(solution)/shard_map/pallas_call | solution.py:95
  186.0 2.8 multiply_reduce_fusion.12
  188.8 5.7 %shard_map.279 = f32[2,128]{1,0:T(2,128)} custom-call(f32[2,128]{1,0:T(2,128)} %bitcast.504), custom_call_target="tpu_custom_call" | custom-call | tf_op jit(solution)/shard_map/pallas_call | solution.py:95
  195.2 3.1 multiply_reduce_fusion.10
  199.5 14.9 %shard_map.280 = bf16[8,384,128]{2,1,0:T(8,128)(2,1)} custom-call(bf16[384,128]{1,0:T(8,128)(2,1)} %bitcast.461), custom_call_target="tpu_custom_call" | custom-call | tf_op jit(solution)/shard_map/pallas_call | solution.py:95
  215.9 2.4 fusion.58
  219.2 2.4 multiply_reduce_fusion.18
  238.8 13.2 %collective-permute-start.3 = (f32[3,640]{1,0:T(4,128)}, f32[3,640]{1,0:T(4,128)}, u32[]{:S(2)}, u32[]{:S(2)}) collective-permute-start(f32[3,640]{1,0:T(4,128)} %pad_add_fusion.3), channel_id=1, source_target_pairs={{4,0},{8,4},{12,8},{16,12},{20,16},{24,20},{28,24},{5,1},{9,5},{13... | collective-permute-start | bytes 23048 | tf_op jit(solution)/shard_map/ppermute | solution.py:130
  254.5 2.3 convolution_convert_fusion.2
  258.7 12.5 %shard_map.278 = f32[64,768]{1,0:T(8,128)} custom-call(bf16[4,64,768]{2,1,0:T(8,128)(2,1)} %bitcast.392), custom_call_target="tpu_custom_call" | custom-call | tf_op jit(solution)/shard_map/pallas_call | solution.py:95
  274.4 2.5 fusion.454
  280.8 14.5 %shard_map.281 = (f32[64,768]{1,0:T(8,128)}, f32[96,384]{1,0:T(8,128)}) custom-call(bf16[4,64,768]{2,1,0:T(8,128)(2,1)} %bitcast.459, bf16[8,96,384]{2,1,0:T(8,128)(2,1)} %bitcast.363), custom_call_target="tpu_custom_call" | custom-call | tf_op jit(solution)/shard_map/pallas_call | solution.py:95
  298.6 19.7 %shard_map.282 = (bf16[4,64,768]{2,1,0:T(8,128)(2,1)}, f32[96,384]{1,0:T(8,128)}, f32[96,384]{1,0:T(8,128)}) custom-call(bf16[64,768]{1,0:T(8,128)(2,1)} %fusion.433.refs_0_, bf16[8,96,384]{2,1,0:T(8,128)(2,1)} %bitcast.367, bf16[8,96,384]{2,1,0:T(8,128)(2,1)} %bitcast.366), custom_call_target="tpu_custom_call" | custom-call | tf_op jit(solution)/shard_map/pallas_call | solution.py:95
  318.4 2.8 multiply_reduce_fusion.13
  323.7 12.2 %shard_map.283 = (f32[2,128]{1,0:T(2,128)}, f32[96,384]{1,0:T(8,128)}) custom-call(f32[2,128]{1,0:T(2,128)} %bitcast.491, bf16[8,96,384]{2,1,0:T(8,128)(2,1)} %pad_maximum_fusion.refs_1_), custom_call_target="tpu_custom_call" | custom-call | tf_op jit(solution)/shard_map/pallas_call | solution.py:95
  336.6 2.2 multiply_reduce_fusion.11
  340.1 13.7 %shard_map.284 = bf16[8,384,128]{2,1,0:T(8,128)(2,1)} custom-call(bf16[384,128]{1,0:T(8,128)(2,1)} %bitcast.460), custom_call_target="tpu_custom_call" | custom-call | tf_op jit(solution)/shard_map/pallas_call | solution.py:95
  355.3 2.3 fusion.60
  358.5 2.3 multiply_reduce_fusion.14
  391.3 14.4 %shard_map.285 = (f32[64,768]{1,0:T(8,128)}, f32[96,384]{1,0:T(8,128)}) custom-call(bf16[4,64,768]{2,1,0:T(8,128)(2,1)} %bitcast.396, bf16[8,96,384]{2,1,0:T(8,128)(2,1)} %bitcast.362), custom_call_target="tpu_custom_call" | custom-call | tf_op jit(solution)/shard_map/pallas_call | solution.py:95
  413.8 29.4 %shard_map.286 = (f32[72,128]{1,0:T(8,128)}, f32[96,384]{1,0:T(8,128)}, f32[96,384]{1,0:T(8,128)}, f32[96,384]{1,0:T(8,128)}) custom-call(f32[72,128]{1,0:T(8,128)} %pad_bitcast_fusion.refs_0_, bf16[8,96,384]{2,1,0:T(8,128)(2,1)} %bitcast.365, bf16[8,96,384]{2,1,0:T(8,128)(2,1)} %bitcast.364, bf16[8,96,384]{2,1,0:T(8,128)(2,1)} %pad_maximum_fusion.1.refs_3_), custom_call_target="tpu_custom_call" | custom-call | tf_op jit(solution)/shard_map/pallas_call | solution.py:95
  445.6 16.1 %shard_map.287 = (f32[4,72,128]{2,1,0:T(8,128)}, f32[2,96,256]{2,1,0:T(8,128)}) custom-call(f32[72,128]{1,0:T(8,128)} %get-tuple-element.60.refs_0_, bf16[2,96,256]{2,1,0:T(8,128)(2,1)} %fusion.131.refs_1_), custom_call_target="tpu_custom_call" | custom-call | tf_op jit(solution)/shard_map/pallas_call | solution.py:95
  (766 shorter events, 153.1 us)
Async XLA Ops:
  7.2 136.9 %all-gather.2.cloned.1.call-start = ((), (), s32[]{:S(2)}) async-start(), calls=%async_computation | async-start | bytes 2654208 | tf_op jit(solution)/shard_map/all_gather | solution.py:253
  42.8 49.5 %copy-start.11 = (f32[256,1152]{1,0:T(8,128)}, f32[256,1152]{1,0:T(8,128)S(1)}, u32[]{:S(2)}) copy-start(f32[256,1152]{1,0:T(8,128)S(1)} %get-tuple-element.328) | copy-start | bytes 3538948
  43.0 21.0 %collective-permute-start = (bf16[3,640]{1,0:T(4,128)(2,1)S(1)}, bf16[3,640]{1,0:T(4,128)(2,1)S(1)}, u32[]{:S(2)}, u32[]{:S(2)}) collective-permute-start(bf16[3,640]{1,0:T(4,128)(2,1)S(1)} %slice.722), channel_id=1, source_target_pairs={{0,4},{4,8},{8,12},{12,16},{16,20},{20,24},{24,28},{1,5},{5,9},{9,... | collective-permute-start | bytes 11528 | tf_op jit(solution)/shard_map/ppermute | solution.py:130
  45.1 13.0 %collective-permute-start.1 = (bf16[3]{0:T(256)(128)(2,1)S(1)}, bf16[3]{0:T(256)(128)(2,1)S(1)}, u32[]{:S(2)}, u32[]{:S(2)}) collective-permute-start(bf16[3]{0:T(256)(128)(2,1)S(1)} %add_convert_fusion.1), channel_id=1, source_target_pairs={{0,4},{4,8},{8,12},{12,16},{16,20},{20,24},{24,28},{1,5},{5,9},{9,... | collective-permute-start | bytes 26 | tf_op jit(solution)/shard_map/ppermute | solution.py:130
  50.9 40.1 %copy-start.81 = (pred[256,256]{1,0:T(8,128)(4,1)}, pred[256,256]{1,0:T(8,128)(4,1)S(1)}, u32[]{:S(2)}) copy-start(pred[256,256]{1,0:T(8,128)(4,1)S(1)} %fusion.122) | copy-start | bytes 196612
  53.0 38.0 %copy-start.79 = (f32[256,6]{0,1:T(8,128)}, f32[256,6]{0,1:T(8,128)S(1)}, u32[]{:S(2)}) copy-start(f32[256,6]{0,1:T(8,128)S(1)} %fusion.121) | copy-start | bytes 18436
  54.5 51.2 %copy-start.84 = (f32[384]{0:T(512)}, f32[384]{0:T(512)S(1)}, u32[]{:S(2)}) copy-start(f32[384]{0:T(512)S(1)} %get-tuple-element.185) | copy-start | bytes 4612
  60.1 86.9 %copy-start.109 = (f32[256]{0:T(256)}, f32[256]{0:T(256)S(1)}, u32[]{:S(2)}) copy-start(f32[256]{0:T(256)S(1)} %get-tuple-element.324) | copy-start | bytes 3076
  60.1 175.3 %copy-start.87 = (f32[256]{0:T(256)}, f32[256]{0:T(256)S(1)}, u32[]{:S(2)}) copy-start(f32[256]{0:T(256)S(1)} %get-tuple-element.310) | copy-start | bytes 3076
  60.1 175.3 %copy-start.89 = (f32[256]{0:T(256)}, f32[256]{0:T(256)S(1)}, u32[]{:S(2)}) copy-start(f32[256]{0:T(256)S(1)} %get-tuple-element.311) | copy-start | bytes 3076
  60.1 175.3 %copy-start.91 = (f32[256]{0:T(256)}, f32[256]{0:T(256)S(1)}, u32[]{:S(2)}) copy-start(f32[256]{0:T(256)S(1)} %get-tuple-element.312) | copy-start | bytes 3076
  87.8 54.9 %copy-start.186 = (f32[6]{0:T(128)}, f32[6]{0:T(128)S(1)}, u32[]{:S(2)}) copy-start(f32[6]{0:T(128)S(1)} %get-tuple-element.296) | copy-start | bytes 76
  88.7 48.7 %copy-start.143 = (f32[6]{0:T(128)}, f32[6]{0:T(128)S(1)}, u32[]{:S(2)}) copy-start(f32[6]{0:T(128)S(1)} %get-tuple-element.289) | copy-start | bytes 76
  88.7 49.5 %copy-start.145 = (f32[6]{0:T(128)}, f32[6]{0:T(128)S(1)}, u32[]{:S(2)}) copy-start(f32[6]{0:T(128)S(1)} %get-tuple-element.290) | copy-start | bytes 76
  88.7 50.2 %copy-start.147 = (f32[6]{0:T(128)}, f32[6]{0:T(128)S(1)}, u32[]{:S(2)}) copy-start(f32[6]{0:T(128)S(1)} %get-tuple-element.291) | copy-start | bytes 76
  88.8 50.9 %copy-start.149 = (f32[6]{0:T(128)}, f32[6]{0:T(128)S(1)}, u32[]{:S(2)}) copy-start(f32[6]{0:T(128)S(1)} %get-tuple-element.292) | copy-start | bytes 76
  88.8 51.7 %copy-start.151 = (f32[6]{0:T(128)}, f32[6]{0:T(128)S(1)}, u32[]{:S(2)}) copy-start(f32[6]{0:T(128)S(1)} %get-tuple-element.293) | copy-start | bytes 76
  88.8 52.4 %copy-start.153 = (f32[6]{0:T(128)}, f32[6]{0:T(128)S(1)}, u32[]{:S(2)}) copy-start(f32[6]{0:T(128)S(1)} %get-tuple-element.294) | copy-start | bytes 76
  88.8 54.6 %copy-start.182 = (f32[6]{0:T(128)}, f32[6]{0:T(128)S(1)}, u32[]{:S(2)}) copy-start(f32[6]{0:T(128)S(1)} %get-tuple-element.288) | copy-start | bytes 76
  93.2 43.6 %copy-start.1 = (f32[256,384]{1,0:T(8,128)}, f32[256,384]{1,0:T(8,128)S(1)}, u32[]{:S(2)}) copy-start(f32[256,384]{1,0:T(8,128)S(1)} %get-tuple-element.211) | copy-start | bytes 1179652
  122.3 174.6 %copy-start.9 = (f32[64,768]{1,0:T(8,128)}, f32[64,768]{1,0:T(8,128)S(1)}, u32[]{:S(2)}) copy-start(f32[64,768]{1,0:T(8,128)S(1)} %get-tuple-element.209) | copy-start | bytes 589828
  147.6 6.9 %collective-permute-start.2 = (bf16[3,640]{1,0:T(4,128)(2,1)S(1)}, bf16[3,640]{1,0:T(4,128)(2,1)S(1)}, u32[]{:S(2)}, u32[]{:S(2)}) collective-permute-start(bf16[3,640]{1,0:T(4,128)(2,1)S(1)} %slice.741), channel_id=1, source_target_pairs={{0,4},{4,8},{8,12},{12,16},{16,20},{20,24},{24,28},{1,5},{5,9},{9,... | collective-permute-start | bytes 11528 | tf_op jit(solution)/shard_map/ppermute | solution.py:130
  174.3 43.9 %copy-start.155 = (f32[6]{0:T(128)}, f32[6]{0:T(128)S(1)}, u32[]{:S(2)}) copy-start(f32[6]{0:T(128)S(1)} %get-tuple-element.304) | copy-start | bytes 76
  174.3 43.9 %copy-start.157 = (f32[6]{0:T(128)}, f32[6]{0:T(128)S(1)}, u32[]{:S(2)}) copy-start(f32[6]{0:T(128)S(1)} %get-tuple-element.303) | copy-start | bytes 76
  186.0 51.5 %copy-start.119 = (f32[256]{0:T(256)}, f32[256]{0:T(256)S(1)}, u32[]{:S(2)}) copy-start(f32[256]{0:T(256)S(1)} %rsqrt_bitcast_fusion) | copy-start | bytes 3076
  238.8 33.8 %collective-permute-start.3 = (f32[3,640]{1,0:T(4,128)}, f32[3,640]{1,0:T(4,128)}, u32[]{:S(2)}, u32[]{:S(2)}) collective-permute-start(f32[3,640]{1,0:T(4,128)} %pad_add_fusion.3), channel_id=1, source_target_pairs={{4,0},{8,4},{12,8},{16,12},{20,16},{24,20},{28,24},{5,1},{9,5},{13... | collective-permute-start | bytes 23048 | tf_op jit(solution)/shard_map/ppermute | solution.py:130
  280.8 37.6 %copy-start.85 = (f32[384]{0:T(512)S(1)}, f32[384]{0:T(512)}, u32[]{:S(2)}) copy-start(f32[384]{0:T(512)} %copy-done.84) | copy-start | bytes 4612
  280.8 37.6 %copy-start.113 = (f32[256]{0:T(256)S(1)}, f32[256]{0:T(256)}, u32[]{:S(2)}) copy-start(f32[256]{0:T(256)} %copy-done.112) | copy-start | bytes 3076
  375.3 9.0 %collective-permute-start.4 = (f32[3,640]{1,0:T(4,128)S(1)}, f32[3,640]{1,0:T(4,128)S(1)}, u32[]{:S(2)}, u32[]{:S(2)}) collective-permute-start(f32[3,640]{1,0:T(4,128)S(1)} %pad_add_fusion.2), channel_id=1, source_target_pairs={{4,0},{8,4},{12,8},{16,12},{20,16},{24,20},{28,24},{5,1},{9,5},{13... | collective-permute-start | bytes 23048 | tf_op jit(solution)/shard_map/ppermute | solution.py:130
  413.8 49.3 %copy-start.207 = (f32[64]{0:T(128)S(1)}, f32[64]{0:T(128)}, u32[]{:S(2)}) copy-start(f32[64]{0:T(128)} %get-tuple-element.173) | copy-start | bytes 772
  413.8 49.9 %copy-start.71 = (f32[96,384]{1,0:T(8,128)S(1)}, f32[96,384]{1,0:T(8,128)}, u32[]{:S(2)}) copy-start(f32[96,384]{1,0:T(8,128)} %get-tuple-element.67) | copy-start | bytes 442372
  413.8 49.9 %copy-start.70 = (f32[96,384]{1,0:T(8,128)S(1)}, f32[96,384]{1,0:T(8,128)}, u32[]{:S(2)}) copy-start(f32[96,384]{1,0:T(8,128)} %get-tuple-element.65) | copy-start | bytes 442372
  (202 other events, 1514.6 us)
Sparse Core Ops, SparseCore 0:
  50.3 36.8 all-gather.1
